TPU v7x, 32 devices: a whole 2x2x4 slice. The times are simulated.
32 devices in a mesh: day: 2 (over x), chan: 16 (over z, y, core).
Axes of the slice: x: 2, y: 2, z: 4, core: 2. Of those that a mesh axis runs over, the one named last changes fastest.
Arguments:
- records: bfloat16 [1024, 8, 3000], P(('day', 'chan')), parts along dimension 0, may hold values from -6 to 6
- live_mask: int32 [1024], P(('day', 'chan')), parts along dimension 0, may hold values 0 or 1
- offsets: int32 [16], replicated, may hold values from 1 to 511, as said below
Outputs:
- correlations: bfloat16 [1024, 16, 2048], P(('day', 'chan')), parts along dimension 0
There are 2 independent parts, one for each index of `day`. A program takes and returns all parts, laid end to end along the dimension named above; an argument that names none is the same for every part. Nothing has to cross between parts.
Inputs may be any that keep to these rules, and one draw needn't show every extreme that they name: offsets[k] lies between k * 32 + 1 and (k + 1) * 32, and the last one equals 511.
All inputs are finite; a program needn't handle non-finite values. No bound on the sum of `live_mask` on one device may be relied on, other than what follows from the above.
Results may differ from a plain program's by a relative error of at most 0.0076.
Values may be sent and summed in bfloat16 or wider, within the bound.
A program may use at most 128 MiB of HBM per device.

v0:
```python
import math

import jax
import jax.numpy as jnp
from jax import lax
from jax.sharding import PartitionSpec as P

F = 512
F0 = 6
LAGS = 2048
BAND = 512


def passed_along(value, axis, by):
    length = lax.axis_size(axis)
    pairs = [(i, i + by) for i in range(length) if 0 <= i + by < length]
    return lax.ppermute(value, axis, pairs)


def forward_table(length):
    samples = jnp.arange(length, dtype=jnp.int32)
    freqs = F0 + jnp.arange(F, dtype=jnp.int32)
    phase = jnp.mod(samples[:, None] * freqs[None, :], length).astype(jnp.float32)
    angle = 2.0 * math.pi / length * phase
    return jnp.concatenate([jnp.cos(angle), -jnp.sin(angle)], axis=1).astype(jnp.bfloat16)


def inverse_table(length):
    freqs = F0 + jnp.arange(F, dtype=jnp.int32)
    shifts = jnp.arange(LAGS, dtype=jnp.int32) - LAGS // 2
    phase = jnp.mod(freqs[:, None] * shifts[None, :], length).astype(jnp.float32)
    angle = 2.0 * math.pi / length * phase
    return jnp.concatenate([jnp.cos(angle), -jnp.sin(angle)], axis=0).astype(jnp.bfloat16)


def whiten(records, live_mask):
    count, windows, length = records.shape
    table = forward_table(length)
    spectrum = jnp.dot(
        records.reshape(count * windows, length), table, preferred_element_type=jnp.float32
    )
    power = jnp.mean(spectrum * spectrum, axis=1, keepdims=True)
    gain = jnp.repeat(live_mask.astype(jnp.float32), windows)[:, None]
    white = spectrum * (gain * lax.rsqrt(power + 1e-06))
    return white.astype(jnp.bfloat16).reshape(count, windows, 2, spectrum.shape[1] // 2)


def stacked_cross(local_spec, extended, offsets):
    row_count, windows, paired, bin_count = local_spec.shape
    first = local_spec.astype(jnp.float32)

    def single(offset_value):
        partner = lax.dynamic_slice_in_dim(extended, offset_value, row_count, 0).astype(jnp.float32)
        real_part = jnp.sum(
            first[:, :, 0] * partner[:, :, 0] + first[:, :, 1] * partner[:, :, 1], axis=1
        )
        imag_part = jnp.sum(
            first[:, :, 1] * partner[:, :, 0] - first[:, :, 0] * partner[:, :, 1], axis=1
        )
        return jnp.stack([real_part, imag_part], axis=1) / float(windows)

    def grouped(group):
        return jax.vmap(single)(group)

    result = lax.map(grouped, offsets.reshape(-1, 8))
    result = result.reshape(offsets.shape[0], row_count, 2, bin_count)
    return jnp.transpose(result, (1, 0, 2, 3)).astype(jnp.bfloat16)


def lag_transform(cross, length):
    count, pairs, paired, bin_count = cross.shape
    table = inverse_table(length)
    result = jnp.dot(
        cross.reshape(count * pairs, 2 * bin_count), table, preferred_element_type=jnp.float32
    )
    result = result * (1.0 / math.sqrt(bin_count))
    return result.reshape(count, pairs, table.shape[1]).astype(jnp.bfloat16)


def shards(records, live_mask, offsets):
    count = records.shape[0]
    spectra = whiten(records, live_mask)
    reach = (BAND + count - 2) // count
    extended = jnp.zeros(((reach + 1) * count,) + spectra.shape[1:], jnp.bfloat16)
    extended = lax.dynamic_update_slice_in_dim(extended, spectra, 0, 0)

    def advance(step_index, carry):
        buffer, travelling = carry
        travelling = passed_along(travelling, "chan", -1)
        buffer = lax.dynamic_update_slice_in_dim(buffer, travelling, step_index * count, 0)
        return (buffer, travelling)

    extended, last_piece = lax.fori_loop(1, reach + 1, advance, (extended, spectra))
    cross = stacked_cross(spectra, extended, offsets)
    return lag_transform(cross, records.shape[2])


def solution(mesh):
    in_specs = (P(("day", "chan"), None, None), P(("day", "chan")), P())
    out_specs = P(("day", "chan"), None, None)
    return jax.shard_map(shards, mesh=mesh, in_specs=in_specs, out_specs=out_specs, check_vma=False)
```

profile of v0, /device:TPU:13, one launch (start us, length us, event | category | flops | bytes accessed | tf_op | source)
XLA Modules:
  0.0 317.9 jit_solution(9821043525393969551)
XLA Ops:
  0.0 26.1 %cosine_convert_fusion = (bf16[3000,512]{1,0:T(8,128)(2,1)S(1)}, bf16[3000,512]{1,0:T(8,128)(2,1)S(1)}) fusion(s32[512]{0:T(512)S(1)} %iota_add_fusion.1), kind=kLoop, calls=%fused_computation.23 | loop fusion | flops 18432000 | bytes 6146048 | tf_op jit(solution)/shard_map/convert.2
  29.0 13.7 %dynamic_update_slice.14 = bf16[544,8,2,512]{3,2,1,0:T(2,128)(2,1)} pad(bf16[32,8,2,512]{3,2,1,0:T(2,128)(2,1)S(1)} %reshape.105, bf16[]{:T(256)} %constant.84.clone.1), padding=0_512x0_0x0_0x0_0 | pad | bytes 9437186 | tf_op jit(solution)/shard_map/dynamic_update_slice | solution.py:85
  43.1 209.4 %while.25 = (s32[]{:T(128)}, bf16[544,8,2,512]{3,2,1,0:T(2,128)(2,1)}, bf16[32,8,2,512]{3,2,1,0:T(2,128)(2,1)S(1)}, s32[]{:T(128)}, s32[]{:T(128)}, /*index=5*/s32[]{:T(128)}, s32[]{:T(128)}) while((s32[]{:T(128)}, bf16[544,8,2,512]{3,2,1,0:T(2,128)(2,1)}, bf16[32,8,2,512]{3,2,1,0:T(2,128)(2,1)S(1)}, s32[]{:T(128)}, s32[]{:T(128)}, ...), condition=%wide.region_2.3_spmd, body=%wide.region_1.2_spmd.sunk | while | flops 6 | bytes 4194471 | solution.py:93
  45.7 8.8 %collective-permute-done = bf16[32,8,2,512]{3,2,1,0:T(2,128)(2,1)S(1)} collective-permute-done((bf16[32,8,2,512]{3,2,1,0:T(2,128)(2,1)S(1)}, bf16[32,8,2,512]{3,2,1,0:T(2,128)(2,1)S(1)}, u32[]{:S(2)}, u32[]{:S(2)}) %collective-permute-start) | collective-permute-done | bytes 524320 | tf_op jit(solution)/shard_map/while/body/eval_jaxpr/ppermute | solution.py:17
  58.1 9.5 %collective-permute-done = bf16[32,8,2,512]{3,2,1,0:T(2,128)(2,1)S(1)} collective-permute-done((bf16[32,8,2,512]{3,2,1,0:T(2,128)(2,1)S(1)}, bf16[32,8,2,512]{3,2,1,0:T(2,128)(2,1)S(1)}, u32[]{:S(2)}, u32[]{:S(2)}) %collective-permute-start) | collective-permute-done | bytes 524320 | tf_op jit(solution)/shard_map/while/body/eval_jaxpr/ppermute | solution.py:17
  71.2 9.5 %collective-permute-done = bf16[32,8,2,512]{3,2,1,0:T(2,128)(2,1)S(1)} collective-permute-done((bf16[32,8,2,512]{3,2,1,0:T(2,128)(2,1)S(1)}, bf16[32,8,2,512]{3,2,1,0:T(2,128)(2,1)S(1)}, u32[]{:S(2)}, u32[]{:S(2)}) %collective-permute-start) | collective-permute-done | bytes 524320 | tf_op jit(solution)/shard_map/while/body/eval_jaxpr/ppermute | solution.py:17
  84.3 9.5 %collective-permute-done = bf16[32,8,2,512]{3,2,1,0:T(2,128)(2,1)S(1)} collective-permute-done((bf16[32,8,2,512]{3,2,1,0:T(2,128)(2,1)S(1)}, bf16[32,8,2,512]{3,2,1,0:T(2,128)(2,1)S(1)}, u32[]{:S(2)}, u32[]{:S(2)}) %collective-permute-start) | collective-permute-done | bytes 524320 | tf_op jit(solution)/shard_map/while/body/eval_jaxpr/ppermute | solution.py:17
  97.4 9.5 %collective-permute-done = bf16[32,8,2,512]{3,2,1,0:T(2,128)(2,1)S(1)} collective-permute-done((bf16[32,8,2,512]{3,2,1,0:T(2,128)(2,1)S(1)}, bf16[32,8,2,512]{3,2,1,0:T(2,128)(2,1)S(1)}, u32[]{:S(2)}, u32[]{:S(2)}) %collective-permute-start) | collective-permute-done | bytes 524320 | tf_op jit(solution)/shard_map/while/body/eval_jaxpr/ppermute | solution.py:17
  110.5 9.5 %collective-permute-done = bf16[32,8,2,512]{3,2,1,0:T(2,128)(2,1)S(1)} collective-permute-done((bf16[32,8,2,512]{3,2,1,0:T(2,128)(2,1)S(1)}, bf16[32,8,2,512]{3,2,1,0:T(2,128)(2,1)S(1)}, u32[]{:S(2)}, u32[]{:S(2)}) %collective-permute-start) | collective-permute-done | bytes 524320 | tf_op jit(solution)/shard_map/while/body/eval_jaxpr/ppermute | solution.py:17
  123.6 9.5 %collective-permute-done = bf16[32,8,2,512]{3,2,1,0:T(2,128)(2,1)S(1)} collective-permute-done((bf16[32,8,2,512]{3,2,1,0:T(2,128)(2,1)S(1)}, bf16[32,8,2,512]{3,2,1,0:T(2,128)(2,1)S(1)}, u32[]{:S(2)}, u32[]{:S(2)}) %collective-permute-start) | collective-permute-done | bytes 524320 | tf_op jit(solution)/shard_map/while/body/eval_jaxpr/ppermute | solution.py:17
  136.7 9.5 %collective-permute-done = bf16[32,8,2,512]{3,2,1,0:T(2,128)(2,1)S(1)} collective-permute-done((bf16[32,8,2,512]{3,2,1,0:T(2,128)(2,1)S(1)}, bf16[32,8,2,512]{3,2,1,0:T(2,128)(2,1)S(1)}, u32[]{:S(2)}, u32[]{:S(2)}) %collective-permute-start) | collective-permute-done | bytes 524320 | tf_op jit(solution)/shard_map/while/body/eval_jaxpr/ppermute | solution.py:17
  149.8 9.5 %collective-permute-done = bf16[32,8,2,512]{3,2,1,0:T(2,128)(2,1)S(1)} collective-permute-done((bf16[32,8,2,512]{3,2,1,0:T(2,128)(2,1)S(1)}, bf16[32,8,2,512]{3,2,1,0:T(2,128)(2,1)S(1)}, u32[]{:S(2)}, u32[]{:S(2)}) %collective-permute-start) | collective-permute-done | bytes 524320 | tf_op jit(solution)/shard_map/while/body/eval_jaxpr/ppermute | solution.py:17
  162.8 9.5 %collective-permute-done = bf16[32,8,2,512]{3,2,1,0:T(2,128)(2,1)S(1)} collective-permute-done((bf16[32,8,2,512]{3,2,1,0:T(2,128)(2,1)S(1)}, bf16[32,8,2,512]{3,2,1,0:T(2,128)(2,1)S(1)}, u32[]{:S(2)}, u32[]{:S(2)}) %collective-permute-start) | collective-permute-done | bytes 524320 | tf_op jit(solution)/shard_map/while/body/eval_jaxpr/ppermute | solution.py:17
  175.9 9.5 %collective-permute-done = bf16[32,8,2,512]{3,2,1,0:T(2,128)(2,1)S(1)} collective-permute-done((bf16[32,8,2,512]{3,2,1,0:T(2,128)(2,1)S(1)}, bf16[32,8,2,512]{3,2,1,0:T(2,128)(2,1)S(1)}, u32[]{:S(2)}, u32[]{:S(2)}) %collective-permute-start) | collective-permute-done | bytes 524320 | tf_op jit(solution)/shard_map/while/body/eval_jaxpr/ppermute | solution.py:17
  189.0 9.5 %collective-permute-done = bf16[32,8,2,512]{3,2,1,0:T(2,128)(2,1)S(1)} collective-permute-done((bf16[32,8,2,512]{3,2,1,0:T(2,128)(2,1)S(1)}, bf16[32,8,2,512]{3,2,1,0:T(2,128)(2,1)S(1)}, u32[]{:S(2)}, u32[]{:S(2)}) %collective-permute-start) | collective-permute-done | bytes 524320 | tf_op jit(solution)/shard_map/while/body/eval_jaxpr/ppermute | solution.py:17
  202.1 9.5 %collective-permute-done = bf16[32,8,2,512]{3,2,1,0:T(2,128)(2,1)S(1)} collective-permute-done((bf16[32,8,2,512]{3,2,1,0:T(2,128)(2,1)S(1)}, bf16[32,8,2,512]{3,2,1,0:T(2,128)(2,1)S(1)}, u32[]{:S(2)}, u32[]{:S(2)}) %collective-permute-start) | collective-permute-done | bytes 524320 | tf_op jit(solution)/shard_map/while/body/eval_jaxpr/ppermute | solution.py:17
  215.2 9.5 %collective-permute-done = bf16[32,8,2,512]{3,2,1,0:T(2,128)(2,1)S(1)} collective-permute-done((bf16[32,8,2,512]{3,2,1,0:T(2,128)(2,1)S(1)}, bf16[32,8,2,512]{3,2,1,0:T(2,128)(2,1)S(1)}, u32[]{:S(2)}, u32[]{:S(2)}) %collective-permute-start) | collective-permute-done | bytes 524320 | tf_op jit(solution)/shard_map/while/body/eval_jaxpr/ppermute | solution.py:17
  228.3 9.5 %collective-permute-done = bf16[32,8,2,512]{3,2,1,0:T(2,128)(2,1)S(1)} collective-permute-done((bf16[32,8,2,512]{3,2,1,0:T(2,128)(2,1)S(1)}, bf16[32,8,2,512]{3,2,1,0:T(2,128)(2,1)S(1)}, u32[]{:S(2)}, u32[]{:S(2)}) %collective-permute-start) | collective-permute-done | bytes 524320 | tf_op jit(solution)/shard_map/while/body/eval_jaxpr/ppermute | solution.py:17
  241.4 9.5 %collective-permute-done = bf16[32,8,2,512]{3,2,1,0:T(2,128)(2,1)S(1)} collective-permute-done((bf16[32,8,2,512]{3,2,1,0:T(2,128)(2,1)S(1)}, bf16[32,8,2,512]{3,2,1,0:T(2,128)(2,1)S(1)}, u32[]{:S(2)}, u32[]{:S(2)}) %collective-permute-start) | collective-permute-done | bytes 524320 | tf_op jit(solution)/shard_map/while/body/eval_jaxpr/ppermute | solution.py:17
  252.6 9.8 %copy.12 = bf16[544,8,2,512]{3,1,2,0:T(8,128)(2,1)} copy(bf16[544,8,2,512]{3,2,1,0:T(2,128)(2,1)} %get-tuple-element.110) | data formatting | bytes 17825792 | tf_op jit(solution)/shard_map/while | solution.py:65
  262.6 31.2 %while.26 = (s32[]{:T(128)}, bf16[2,8,32,2,512]{4,3,2,1,0:T(2,128)(2,1)}, f32[32,8,2,512]{3,1,0,2:T(8,128)S(1)}, s32[2,8]{1,0:T(2,128)S(1)}, bf16[544,8,2,512]{3,1,2,0:T(8,128)(2,1)}, /*index=5*/s32[]{:T(128)}) while((s32[]{:T(128)}, bf16[2,8,32,2,512]{4,3,2,1,0:T(2,128)(2,1)}, f32[32,8,2,512]{3,1,0,2:T(8,128)S(1)}, s32[2,8]{1,0:T(2,128)S(1)}, ...), condition=%wide.region_6.7_spmd, body=%wide.region_3.6_spmd.sunk | while | flops 10747946 | bytes 37749512 | solution.py:65
  262.8 6.3 %gather_fusion = bf16[8,32,8,2,512]{4,2,3,1,0:T(8,128)(2,1)} fusion(bf16[544,8,2,512]{3,1,2,0:T(8,128)(2,1)} %get-tuple-element.232, s32[8]{0:T(128)S(1)} %fusion.31), kind=kCustom, calls=%fused_computation.clone.1 | custom fusion | bytes 8388736 | tf_op jit(solution)/shard_map/while/body/eval_jaxpr/vmap()/gather | solution.py:53
  278.3 6.3 %gather_fusion = bf16[8,32,8,2,512]{4,2,3,1,0:T(8,128)(2,1)} fusion(bf16[544,8,2,512]{3,1,2,0:T(8,128)(2,1)} %get-tuple-element.232, s32[8]{0:T(128)S(1)} %fusion.31), kind=kCustom, calls=%fused_computation.clone.1 | custom fusion | bytes 8388736 | tf_op jit(solution)/shard_map/while/body/eval_jaxpr/vmap()/gather | solution.py:53
  296.4 17.8 %cosine_convert_fusion.1 = (bf16[512,2048]{1,0:T(8,128)(2,1)S(1)}, bf16[512,2048]{1,0:T(8,128)(2,1)S(1)}) fusion(s32[2048]{0:T(1024)S(1)} %iota_add_fusion, s32[512]{0:T(512)S(1)} %iota_add_fusion.1), kind=kLoop, calls=%fused_computation.36 | loop fusion | flops 12582912 | bytes 4204544 | tf_op jit(solution)/shard_map/convert
  (85 shorter events, 86.4 us)
Async XLA Ops:
  0.0 26.1 %copy-start = (bf16[32,8,3000]{2,1,0:T(8,128)(2,1)S(1)}, bf16[32,8,3000]{2,1,0:T(8,128)(2,1)}, u32[]{:S(2)}) copy-start(bf16[32,8,3000]{2,1,0:T(8,128)(2,1)} %param.7) | copy-start | bytes 4608004
  26.1 2.0 copy-start.1
  43.1 11.4 %collective-permute-start = (bf16[32,8,2,512]{3,2,1,0:T(2,128)(2,1)S(1)}, bf16[32,8,2,512]{3,2,1,0:T(2,128)(2,1)S(1)}, u32[]{:S(2)}, u32[]{:S(2)}) collective-permute-start(bf16[32,8,2,512]{3,2,1,0:T(2,128)(2,1)S(1)} %get-tuple-element.204), channel_id=1, source_target_pairs={{1,0},{2,1},{3,2},{4,3},{5,4},{6,5},{7,6},{8,7},{9,8},{10,9},{11,1... | collective-permute-start | bytes 1572872 | tf_op jit(solution)/shard_map/while/body/eval_jaxpr/ppermute | solution.py:17
  56.2 11.4 %collective-permute-start = (bf16[32,8,2,512]{3,2,1,0:T(2,128)(2,1)S(1)}, bf16[32,8,2,512]{3,2,1,0:T(2,128)(2,1)S(1)}, u32[]{:S(2)}, u32[]{:S(2)}) collective-permute-start(bf16[32,8,2,512]{3,2,1,0:T(2,128)(2,1)S(1)} %get-tuple-element.204), channel_id=1, source_target_pairs={{1,0},{2,1},{3,2},{4,3},{5,4},{6,5},{7,6},{8,7},{9,8},{10,9},{11,1... | collective-permute-start | bytes 1572872 | tf_op jit(solution)/shard_map/while/body/eval_jaxpr/ppermute | solution.py:17
  69.3 11.4 %collective-permute-start = (bf16[32,8,2,512]{3,2,1,0:T(2,128)(2,1)S(1)}, bf16[32,8,2,512]{3,2,1,0:T(2,128)(2,1)S(1)}, u32[]{:S(2)}, u32[]{:S(2)}) collective-permute-start(bf16[32,8,2,512]{3,2,1,0:T(2,128)(2,1)S(1)} %get-tuple-element.204), channel_id=1, source_target_pairs={{1,0},{2,1},{3,2},{4,3},{5,4},{6,5},{7,6},{8,7},{9,8},{10,9},{11,1... | collective-permute-start | bytes 1572872 | tf_op jit(solution)/shard_map/while/body/eval_jaxpr/ppermute | solution.py:17
  82.4 11.4 %collective-permute-start = (bf16[32,8,2,512]{3,2,1,0:T(2,128)(2,1)S(1)}, bf16[32,8,2,512]{3,2,1,0:T(2,128)(2,1)S(1)}, u32[]{:S(2)}, u32[]{:S(2)}) collective-permute-start(bf16[32,8,2,512]{3,2,1,0:T(2,128)(2,1)S(1)} %get-tuple-element.204), channel_id=1, source_target_pairs={{1,0},{2,1},{3,2},{4,3},{5,4},{6,5},{7,6},{8,7},{9,8},{10,9},{11,1... | collective-permute-start | bytes 1572872 | tf_op jit(solution)/shard_map/while/body/eval_jaxpr/ppermute | solution.py:17
  95.5 11.4 %collective-permute-start = (bf16[32,8,2,512]{3,2,1,0:T(2,128)(2,1)S(1)}, bf16[32,8,2,512]{3,2,1,0:T(2,128)(2,1)S(1)}, u32[]{:S(2)}, u32[]{:S(2)}) collective-permute-start(bf16[32,8,2,512]{3,2,1,0:T(2,128)(2,1)S(1)} %get-tuple-element.204), channel_id=1, source_target_pairs={{1,0},{2,1},{3,2},{4,3},{5,4},{6,5},{7,6},{8,7},{9,8},{10,9},{11,1... | collective-permute-start | bytes 1572872 | tf_op jit(solution)/shard_map/while/body/eval_jaxpr/ppermute | solution.py:17
  108.5 11.4 %collective-permute-start = (bf16[32,8,2,512]{3,2,1,0:T(2,128)(2,1)S(1)}, bf16[32,8,2,512]{3,2,1,0:T(2,128)(2,1)S(1)}, u32[]{:S(2)}, u32[]{:S(2)}) collective-permute-start(bf16[32,8,2,512]{3,2,1,0:T(2,128)(2,1)S(1)} %get-tuple-element.204), channel_id=1, source_target_pairs={{1,0},{2,1},{3,2},{4,3},{5,4},{6,5},{7,6},{8,7},{9,8},{10,9},{11,1... | collective-permute-start | bytes 1572872 | tf_op jit(solution)/shard_map/while/body/eval_jaxpr/ppermute | solution.py:17
  121.6 11.4 %collective-permute-start = (bf16[32,8,2,512]{3,2,1,0:T(2,128)(2,1)S(1)}, bf16[32,8,2,512]{3,2,1,0:T(2,128)(2,1)S(1)}, u32[]{:S(2)}, u32[]{:S(2)}) collective-permute-start(bf16[32,8,2,512]{3,2,1,0:T(2,128)(2,1)S(1)} %get-tuple-element.204), channel_id=1, source_target_pairs={{1,0},{2,1},{3,2},{4,3},{5,4},{6,5},{7,6},{8,7},{9,8},{10,9},{11,1... | collective-permute-start | bytes 1572872 | tf_op jit(solution)/shard_map/while/body/eval_jaxpr/ppermute | solution.py:17
  134.7 11.4 %collective-permute-start = (bf16[32,8,2,512]{3,2,1,0:T(2,128)(2,1)S(1)}, bf16[32,8,2,512]{3,2,1,0:T(2,128)(2,1)S(1)}, u32[]{:S(2)}, u32[]{:S(2)}) collective-permute-start(bf16[32,8,2,512]{3,2,1,0:T(2,128)(2,1)S(1)} %get-tuple-element.204), channel_id=1, source_target_pairs={{1,0},{2,1},{3,2},{4,3},{5,4},{6,5},{7,6},{8,7},{9,8},{10,9},{11,1... | collective-permute-start | bytes 1572872 | tf_op jit(solution)/shard_map/while/body/eval_jaxpr/ppermute | solution.py:17
  147.9 11.4 %collective-permute-start = (bf16[32,8,2,512]{3,2,1,0:T(2,128)(2,1)S(1)}, bf16[32,8,2,512]{3,2,1,0:T(2,128)(2,1)S(1)}, u32[]{:S(2)}, u32[]{:S(2)}) collective-permute-start(bf16[32,8,2,512]{3,2,1,0:T(2,128)(2,1)S(1)} %get-tuple-element.204), channel_id=1, source_target_pairs={{1,0},{2,1},{3,2},{4,3},{5,4},{6,5},{7,6},{8,7},{9,8},{10,9},{11,1... | collective-permute-start | bytes 1572872 | tf_op jit(solution)/shard_map/while/body/eval_jaxpr/ppermute | solution.py:17
  160.9 11.4 %collective-permute-start = (bf16[32,8,2,512]{3,2,1,0:T(2,128)(2,1)S(1)}, bf16[32,8,2,512]{3,2,1,0:T(2,128)(2,1)S(1)}, u32[]{:S(2)}, u32[]{:S(2)}) collective-permute-start(bf16[32,8,2,512]{3,2,1,0:T(2,128)(2,1)S(1)} %get-tuple-element.204), channel_id=1, source_target_pairs={{1,0},{2,1},{3,2},{4,3},{5,4},{6,5},{7,6},{8,7},{9,8},{10,9},{11,1... | collective-permute-start | bytes 1572872 | tf_op jit(solution)/shard_map/while/body/eval_jaxpr/ppermute | solution.py:17
  174.0 11.4 %collective-permute-start = (bf16[32,8,2,512]{3,2,1,0:T(2,128)(2,1)S(1)}, bf16[32,8,2,512]{3,2,1,0:T(2,128)(2,1)S(1)}, u32[]{:S(2)}, u32[]{:S(2)}) collective-permute-start(bf16[32,8,2,512]{3,2,1,0:T(2,128)(2,1)S(1)} %get-tuple-element.204), channel_id=1, source_target_pairs={{1,0},{2,1},{3,2},{4,3},{5,4},{6,5},{7,6},{8,7},{9,8},{10,9},{11,1... | collective-permute-start | bytes 1572872 | tf_op jit(solution)/shard_map/while/body/eval_jaxpr/ppermute | solution.py:17
  187.1 11.4 %collective-permute-start = (bf16[32,8,2,512]{3,2,1,0:T(2,128)(2,1)S(1)}, bf16[32,8,2,512]{3,2,1,0:T(2,128)(2,1)S(1)}, u32[]{:S(2)}, u32[]{:S(2)}) collective-permute-start(bf16[32,8,2,512]{3,2,1,0:T(2,128)(2,1)S(1)} %get-tuple-element.204), channel_id=1, source_target_pairs={{1,0},{2,1},{3,2},{4,3},{5,4},{6,5},{7,6},{8,7},{9,8},{10,9},{11,1... | collective-permute-start | bytes 1572872 | tf_op jit(solution)/shard_map/while/body/eval_jaxpr/ppermute | solution.py:17
  200.2 11.4 %collective-permute-start = (bf16[32,8,2,512]{3,2,1,0:T(2,128)(2,1)S(1)}, bf16[32,8,2,512]{3,2,1,0:T(2,128)(2,1)S(1)}, u32[]{:S(2)}, u32[]{:S(2)}) collective-permute-start(bf16[32,8,2,512]{3,2,1,0:T(2,128)(2,1)S(1)} %get-tuple-element.204), channel_id=1, source_target_pairs={{1,0},{2,1},{3,2},{4,3},{5,4},{6,5},{7,6},{8,7},{9,8},{10,9},{11,1... | collective-permute-start | bytes 1572872 | tf_op jit(solution)/shard_map/while/body/eval_jaxpr/ppermute | solution.py:17
  213.3 11.4 %collective-permute-start = (bf16[32,8,2,512]{3,2,1,0:T(2,128)(2,1)S(1)}, bf16[32,8,2,512]{3,2,1,0:T(2,128)(2,1)S(1)}, u32[]{:S(2)}, u32[]{:S(2)}) collective-permute-start(bf16[32,8,2,512]{3,2,1,0:T(2,128)(2,1)S(1)} %get-tuple-element.204), channel_id=1, source_target_pairs={{1,0},{2,1},{3,2},{4,3},{5,4},{6,5},{7,6},{8,7},{9,8},{10,9},{11,1... | collective-permute-start | bytes 1572872 | tf_op jit(solution)/shard_map/while/body/eval_jaxpr/ppermute | solution.py:17
  226.4 11.4 %collective-permute-start = (bf16[32,8,2,512]{3,2,1,0:T(2,128)(2,1)S(1)}, bf16[32,8,2,512]{3,2,1,0:T(2,128)(2,1)S(1)}, u32[]{:S(2)}, u32[]{:S(2)}) collective-permute-start(bf16[32,8,2,512]{3,2,1,0:T(2,128)(2,1)S(1)} %get-tuple-element.204), channel_id=1, source_target_pairs={{1,0},{2,1},{3,2},{4,3},{5,4},{6,5},{7,6},{8,7},{9,8},{10,9},{11,1... | collective-permute-start | bytes 1572872 | tf_op jit(solution)/shard_map/while/body/eval_jaxpr/ppermute | solution.py:17
  239.5 11.4 %collective-permute-start = (bf16[32,8,2,512]{3,2,1,0:T(2,128)(2,1)S(1)}, bf16[32,8,2,512]{3,2,1,0:T(2,128)(2,1)S(1)}, u32[]{:S(2)}, u32[]{:S(2)}) collective-permute-start(bf16[32,8,2,512]{3,2,1,0:T(2,128)(2,1)S(1)} %get-tuple-element.204), channel_id=1, source_target_pairs={{1,0},{2,1},{3,2},{4,3},{5,4},{6,5},{7,6},{8,7},{9,8},{10,9},{11,1... | collective-permute-start | bytes 1572872 | tf_op jit(solution)/shard_map/while/body/eval_jaxpr/ppermute | solution.py:17
  252.5 10.0 %copy-start.2 = (s32[16]{0:T(128)S(1)}, s32[16]{0:T(128)}, u32[]{:S(2)}) copy-start(s32[16]{0:T(128)} %param.9) | copy-start | bytes 196
where the time goes:
time: 319 us; the launch traced here: 318 us
  waiting for transfers between devices  151 us (47%)
  local copies, waits for them, and re-layouts  68.8 us (22%)
  other arithmetic  60.8 us (19%)
  starting transfers between devices  31.2 us (10%)
  matrix products  5.65 us (2%)
    ppermute x16, waiting for transfers between devices, passed_along(): return lax.ppermute(value, axis, pairs)  151 us
    another operation x2, other arithmetic  43.9 us
    ppermute x16, starting transfers between devices, passed_along(): return lax.ppermute(value, axis, pairs)  31.2 us
    dynamic_update_slice x16, local copies, waits for them, and re-layouts, advance(): lax.dynamic_update_slice_in_dim(buffer, travelling, step_index * count, 0)  20.2 us
    dynamic_update_slice x1, local copies, waits for them, and re-layouts, shards(): extended = lax.dynamic_update_slice_in_dim(extended, spectra, 0, 0)  13.7 us
    gather x2, local copies, waits for them, and re-layouts, single(): lax.dynamic_slice_in_dim(extended, offset_value, row_count, 0)  12.7 us
    while x2, local copies, waits for them, and re-layouts, stacked_cross(): result = lax.map(grouped, offsets.reshape(-1, 8))  9.96 us
    while x16, local copies, waits for them, and re-layouts  6.93 us
  transfers between devices with their start and end apart: 16, of which 16 were waited for; matrix products, arithmetic and copies ran while one was open for 0% of the time, Pallas kernels for 0%

commit v1 on v0

v1 whole, which is shorter than its diff:
```python
import functools
import math

import jax
import jax.numpy as jnp
import numpy as np
from jax import lax
from jax.experimental import pallas as pl
from jax.experimental.pallas import tpu as pltpu
from jax.sharding import PartitionSpec as P

F = 512
F0 = 6
LAGS = 2048
LANES = 128


def forward_table(length):
    samples = np.arange(length, dtype=np.int64)
    freqs = F0 + np.arange(F, dtype=np.int64)
    phase = np.mod(samples[:, None] * freqs[None, :], length)
    angle = 2.0 * math.pi / length * phase
    return np.concatenate([np.cos(angle), -np.sin(angle)], axis=1).astype(np.float32).astype(jnp.bfloat16)


def inverse_table(length):
    freqs = F0 + np.arange(F, dtype=np.int64)
    shifts = np.arange(LAGS, dtype=np.int64) - LAGS // 2
    phase = np.mod(freqs[:, None] * shifts[None, :], length)
    angle = 2.0 * math.pi / length * phase
    return np.concatenate([np.cos(angle), -np.sin(angle)], axis=0).astype(np.float32).astype(jnp.bfloat16)


def whiten(records, live_mask):
    count, windows, length = records.shape
    spectrum = jnp.dot(
        records.reshape(count * windows, length),
        jnp.asarray(forward_table(length)),
        preferred_element_type=jnp.float32,
    )
    power = jnp.mean(spectrum * spectrum, axis=1, keepdims=True)
    gain = jnp.repeat(live_mask.astype(jnp.float32), windows)[:, None]
    white = spectrum * (gain * lax.rsqrt(power + 1e-06))
    return white.astype(jnp.bfloat16)


def cross_kernel(windows, offsets_ref, all_ref, cross_ref, own, swapped):
    total = all_ref.shape[0]
    count = own.shape[0]
    pairs = offsets_ref.shape[0]
    first = lax.axis_index("chan") * count
    low = lax.broadcasted_iota(jnp.int32, (8, LANES), 0) < 4

    def prepare(c, carry):
        value = all_ref[first + c].astype(jnp.float32)
        own[c] = value
        for w in range(windows):
            swapped[c, w * 8 : w * 8 + 8] = pltpu.roll(value[w * 8 : w * 8 + 8], 4, 0)
        return carry

    lax.fori_loop(0, count, prepare, 0)

    def channel(c, carry):
        mine = own[c]
        turned = swapped[c]
        for k in range(pairs):
            place = first + c + offsets_ref[k]
            keep = jnp.where(place < total, 1.0 / windows, 0.0)
            partner = all_ref[jnp.minimum(place, total - 1)].astype(jnp.float32)
            straight = mine[:8] * partner[:8]
            twisted = turned[:8] * partner[:8]
            for w in range(1, windows):
                rows = slice(w * 8, w * 8 + 8)
                straight += mine[rows] * partner[rows]
                twisted += turned[rows] * partner[rows]
            joined = jnp.where(
                low,
                straight + pltpu.roll(straight, 4, 0),
                pltpu.roll(twisted, 4, 0) - twisted,
            )
            cross_ref[c, k] = joined * keep
        return carry

    lax.fori_loop(0, count, channel, 0)


def shards(records, live_mask, offsets):
    count, windows, length = records.shape
    pairs = offsets.shape[0]
    spectra = whiten(records, live_mask).reshape(count, windows * 8, LANES)
    gathered = lax.all_gather(spectra, "chan", axis=0, tiled=True)
    cross = pl.pallas_call(
        functools.partial(cross_kernel, windows),
        out_shape=jax.ShapeDtypeStruct((count, pairs, 8, LANES), jnp.float32),
        in_specs=[
            pl.BlockSpec(memory_space=pltpu.SMEM),
            pl.BlockSpec(memory_space=pltpu.VMEM),
        ],
        out_specs=pl.BlockSpec(memory_space=pltpu.VMEM),
        scratch_shapes=[
            pltpu.VMEM((count, windows * 8, LANES), jnp.float32),
            pltpu.VMEM((count, windows * 8, LANES), jnp.float32),
        ],
        compiler_params=pltpu.CompilerParams(vmem_limit_bytes=40 * 1024 * 1024),
    )(offsets, gathered)
    cross = cross.astype(jnp.bfloat16).reshape(count * pairs, 8 * LANES)
    result = jnp.dot(cross, jnp.asarray(inverse_table(length)), preferred_element_type=jnp.float32)
    result = result * (1.0 / math.sqrt(F))
    return result.reshape(count, pairs, LAGS).astype(jnp.bfloat16)


def solution(mesh):
    in_specs = (P(("day", "chan"), None, None), P(("day", "chan")), P())
    out_specs = P(("day", "chan"), None, None)
    return jax.shard_map(shards, mesh=mesh, in_specs=in_specs, out_specs=out_specs, check_vma=False)
```

time: 319 us -> 110 us (0.34)
  the two profiles are of different devices: /device:TPU:13 before, /device:TPU:1 now
where the time goes in v1:
time: 110 us; the launch traced here: 109 us
  waiting for transfers between devices  76.9 us (70%)
  between operations  13.4 us (12%)
  matrix products  8.36 us (8%)
  local copies, waits for them, and re-layouts  5.26 us (5%)
  Pallas kernels  4.24 us (4%)
    all_gather x1, waiting for transfers between devices, shards(): gathered = lax.all_gather(spectra, 'chan', axis=0, tiled=True)  76.9 us
    dot_general x1, matrix products, whiten(): jnp.dot(records.reshape(count * windows, length), jnp.asarray(forward_tab...  4.68 us
    pallas_call x1, Pallas kernels, shards(): pl.pallas_call(functools.partial(cross_kernel, windows), out_shape=jax.Sh...  4.24 us
    unnamed x8, local copies, waits for them, and re-layouts  3.87 us
    dot_general x1, matrix products, shards(): jnp.dot(cross, jnp.asarray(inverse_table(length)), preferred_element_type...  3.69 us
  transfers between devices with their start and end apart: 1, of which 1 were waited for; matrix products, arithmetic and copies ran while one was open for 0% of the time, Pallas kernels for 0%

profile of v1, /device:TPU:1, one launch (start us, length us, event | category | flops | bytes accessed | tf_op | source)
XLA Modules:
  0.0 109.3 jit_solution(9183969842976751591)
XLA Ops:
  6.5 0.0 copy-start
  6.5 0.0 all-gather.2.cloned.1.call-start
  6.5 0.8 convert_element_type.15
  7.3 0.1 broadcast_in_dim.4
  7.4 0.1 broadcast_in_dim_reshape.3
  7.5 0.5 copy-done
  8.0 4.7 %multiply_reduce_fusion = (f32[256]{0:T(256)S(1)}, f32[1024,256]{1,0:T(8,128)S(1)}) fusion(bf16[3000,1024]{1,0:T(8,128)(2,1)} %constant.13.clone, bf16[32,8,3000]{2,1,0:T(8,128)(2,1)S(1)} %copy-done), kind=kOutput, calls=%fused_computation.6 | convolution fusion | flops 1573388032 | bytes 8729600 | tf_op jit(solution)/shard_map/dot_general | solution.py:36
  12.6 0.0 copy-start.2
  12.7 0.1 fusion.4
  12.8 0.2 copy.8
  13.0 1.0 reshape.27
  14.0 0.0 all-gather.2.cloned.1.call-update
  14.0 76.9 %all-gather.2.cloned.1.call-done.all_ref = bf16[512,64,128]{2,1,0:T(8,128)(2,1)} async-done(((bf16[32,64,128]{2,1,0:T(8,128)(2,1)}), bf16[512,64,128]{2,1,0:T(8,128)(2,1)}) %all-gather.2.cloned.1.call-update) | async-done | bytes 8388624 | tf_op jit(solution)/shard_map/all_gather | solution.py:91
  91.0 0.0 copy-done.2
  91.0 0.0 copy-start.1
  91.0 3.4 %copy-done.1 = bf16[512,64,128]{2,1,0:T(8,128)(2,1)S(1)} copy-done((bf16[512,64,128]{2,1,0:T(8,128)(2,1)S(1)}, bf16[512,64,128]{2,1,0:T(8,128)(2,1)}, u32[]{:S(2)}) %copy-start.1) | copy-done | bytes 8388632
  94.4 0.0 copy-start.3
  94.4 4.2 %shard_map.55 = f32[32,16,8,128]{3,2,1,0:T(8,128)S(1)} custom-call(s32[16]{0:T(128)S(1)} %copy-done.2, bf16[512,64,128]{2,1,0:T(8,128)(2,1)S(1)} %copy-done.1), custom_call_target="tpu_custom_call" | custom-call | tf_op jit(solution)/shard_map/pallas_call | solution.py:92
  98.6 0.2 convert_element_type.17
  98.8 0.0 copy-done.3
  98.8 3.7 %multiply_convert_fusion = bf16[512,2048]{1,0:T(8,128)(2,1)} fusion(bf16[1024,2048]{1,0:T(8,128)(2,1)S(1)} %copy-done.3, bf16[64,8,8,128]{3,2,1,0:T(8,128)(2,1)S(1)} %bitcast.15), kind=kOutput, calls=%fused_computation | convolution fusion | flops 2149580800 | bytes 7340032 | tf_op jit(solution)/shard_map/dot_general | solution.py:107
  (1 shorter events, 0.0 us)
Async XLA Ops:
  6.5 1.4 %copy-start = (bf16[32,8,3000]{2,1,0:T(8,128)(2,1)S(1)}, bf16[32,8,3000]{2,1,0:T(8,128)(2,1)}, u32[]{:S(2)}) copy-start(bf16[32,8,3000]{2,1,0:T(8,128)(2,1)} %param.5) | copy-start | bytes 4608004
  6.5 84.4 %all-gather.2.cloned.1.call-start = ((), (), s32[]{:S(2)}) async-start(), calls=%async_computation | async-start | bytes 8912896 | tf_op jit(solution)/shard_map/all_gather | solution.py:91
  12.6 78.3 %copy-start.2 = (s32[16]{0:T(128)S(1)}, s32[16]{0:T(128)}, u32[]{:S(2)}) copy-start(s32[16]{0:T(128)} %offsets_ref.1) | copy-start | bytes 196
  91.0 3.4 %copy-start.1 = (bf16[512,64,128]{2,1,0:T(8,128)(2,1)S(1)}, bf16[512,64,128]{2,1,0:T(8,128)(2,1)}, u32[]{:S(2)}) copy-start(bf16[512,64,128]{2,1,0:T(8,128)(2,1)} %all-gather.2.cloned.1.call-done.all_ref) | copy-start | bytes 25165828
  94.4 4.4 %copy-start.3 = (bf16[1024,2048]{1,0:T(8,128)(2,1)S(1)}, bf16[1024,2048]{1,0:T(8,128)(2,1)}, u32[]{:S(2)}) copy-start(bf16[1024,2048]{1,0:T(8,128)(2,1)} %constant.14.clone) | copy-start | bytes 12582916
Sparse Core Ops, SparseCore 0:
  14.2 76.7 all-gather.1

commit v2 on v1

v2 whole, which is shorter than its diff:
```python
import functools
import math

import jax
import jax.numpy as jnp
import numpy as np
from jax import lax
from jax.experimental import pallas as pl
from jax.experimental.pallas import tpu as pltpu
from jax.sharding import PartitionSpec as P

F = 512
F0 = 6
LAGS = 2048
LANES = 128
BAND = 512
PIECES = 2
LAYER_CHIPS = 4


def forward_table(length):
    samples = np.arange(length, dtype=np.int64)
    freqs = F0 + np.arange(F, dtype=np.int64)
    phase = np.mod(samples[:, None] * freqs[None, :], length)
    angle = 2.0 * math.pi / length * phase
    return np.concatenate([np.cos(angle), -np.sin(angle)], axis=1).astype(np.float32).astype(jnp.bfloat16)


def inverse_table(length):
    freqs = F0 + np.arange(F, dtype=np.int64)
    shifts = np.arange(LAGS, dtype=np.int64) - LAGS // 2
    phase = np.mod(freqs[:, None] * shifts[None, :], length)
    angle = 2.0 * math.pi / length * phase
    return np.concatenate([np.cos(angle), -np.sin(angle)], axis=0).astype(np.float32).astype(jnp.bfloat16)


def whiten(records, live_mask):
    count, windows, length = records.shape
    spectrum = jnp.dot(
        records.reshape(count * windows, length),
        jnp.asarray(forward_table(length)),
        preferred_element_type=jnp.float32,
    )
    power = jnp.mean(spectrum * spectrum, axis=1, keepdims=True)
    gain = jnp.repeat(live_mask.astype(jnp.float32), windows)[:, None]
    white = spectrum * (gain * lax.rsqrt(power + 1e-06))
    return white.astype(jnp.bfloat16)


def reach_kernel(shape, offsets_ref, white_ref, cross_ref, held, ext, own, swapped,
                 z_send, z_recv, c_send, c_recv, y_send, y_recv, d_send, d_recv):
    layers, columns, depth, pieces, windows = shape
    count, slab = white_ref.shape[0], white_ref.shape[1]
    pairs = offsets_ref.shape[0]
    wide = 2 * columns
    total = layers * wide * count
    me = lax.axis_index("chan")
    z, q = me // wide, me % wide
    y, c = q // 2, q % 2
    sibling = me + 1 - 2 * c
    sib_q = q + 1 - 2 * c
    mate = me + 2 - 4 * y
    mate_q = q + 2 - 4 * y
    far_q = sib_q + 2 - 4 * y
    step = count // pieces

    barrier = pltpu.get_barrier_semaphore()

    def greet(device):
        pl.semaphore_signal(barrier, inc=1, device_id={"chan": device}, device_id_type=pl.DeviceIdType.MESH)

    greet(sibling)
    if columns == 2:
        greet(mate)

    @pl.when(z >= 1)
    def _():
        greet(me - wide)

    @pl.when(z < layers - 1)
    def _():
        greet(me + wide)

    above = jnp.minimum(layers - 1 - z, 1)
    pl.semaphore_wait(barrier, columns + jnp.minimum(z, 1) + above)

    def rows(p):
        return pl.ds(p * step, step)

    def mine(dz, p):
        return white_ref.at[rows(p)] if dz == 0 else held.at[dz * wide + q, rows(p)]

    def copy(source, slot, p, send, recv, device):
        return pltpu.make_async_remote_copy(
            src_ref=source,
            dst_ref=held.at[slot, rows(p)],
            send_sem=send,
            recv_sem=recv,
            device_id={"chan": device},
            device_id_type=pl.DeviceIdType.MESH,
        )

    def down(dz, p):
        return copy(mine(dz, p), (dz + 1) * wide + q, p, z_send.at[dz, p], z_recv.at[dz + 1, p], me - wide)

    def from_above(dz, p):
        return copy(mine(dz, p), dz * wide + q, p, z_send.at[dz, p], z_recv.at[dz, p], me)

    def across(dz, p, slot):
        return copy(mine(dz, p), slot, p, c_send.at[dz, p], c_recv.at[dz, p], sibling)

    def over(dz, p, slot):
        return copy(mine(dz, p), slot, p, y_send.at[dz, p], y_recv.at[dz, p], mate)

    def onward(dz, p, slot):
        return copy(held.at[dz * wide + mate_q, rows(p)], slot, p, d_send.at[dz, p], d_recv.at[dz, p], sibling)

    def both(*conditions):
        joined = conditions[0]
        for condition in conditions[1:]:
            joined = jnp.logical_and(joined, condition)
        return joined

    def exists(dz):
        return z + dz < layers

    def sends(dz):
        for p in range(pieces):
            if dz > 0:
                @pl.when(exists(dz))
                def _():
                    from_above(dz, p).wait_recv()
            if dz < depth:
                @pl.when(both(exists(dz), z >= 1))
                def _():
                    down(dz, p).start()
            if columns == 2:
                @pl.when(both(exists(dz), y == 1) if dz == 0 else exists(dz))
                def _():
                    over(dz, p, dz * wide + q).start()
            @pl.when(both(exists(dz), c == 1) if dz == 0 else exists(dz))
            def _():
                across(dz, p, dz * wide + q).start()

    def passes(dz):
        if columns == 2:
            for p in range(pieces):
                @pl.when(both(exists(dz), y == 0) if dz == 0 else exists(dz))
                def _():
                    over(dz, p, dz * wide + mate_q).wait_recv()
                    onward(dz, p, dz * wide + mate_q).start()

    def arrives(dz):
        for p in range(pieces):
            @pl.when(both(exists(dz), c == 0) if dz == 0 else exists(dz))
            def _():
                across(dz, p, dz * wide + sib_q).wait_recv()
            if columns == 2:
                @pl.when(both(exists(dz), y == 0) if dz == 0 else exists(dz))
                def _():
                    onward(dz, p, dz * wide + far_q).wait_recv()

    def finishes(dz):
        for p in range(pieces):
            if dz < depth:
                @pl.when(both(exists(dz), z >= 1))
                def _():
                    down(dz, p).wait_send()
            if columns == 2:
                @pl.when(both(exists(dz), y == 1) if dz == 0 else exists(dz))
                def _():
                    over(dz, p, dz * wide + q).wait_send()
                @pl.when(both(exists(dz), y == 0) if dz == 0 else exists(dz))
                def _():
                    onward(dz, p, dz * wide + mate_q).wait_send()
            @pl.when(both(exists(dz), c == 1) if dz == 0 else exists(dz))
            def _():
                across(dz, p, dz * wide + q).wait_send()

    low = lax.broadcasted_iota(jnp.int32, (8, LANES), 0) < 4

    def prepare(i, carry):
        raw = white_ref[i]
        value = raw.astype(jnp.float32)
        own[i] = value
        ext[q * count + i] = raw
        for w in range(windows):
            swapped[i, w * 8 : w * 8 + 8] = pltpu.roll(value[w * 8 : w * 8 + 8], 4, 0)
        return carry

    def settle(dz):
        def one(l):
            def fill(i, carry):
                ext[(dz * wide + l) * count + i] = held[dz * wide + l, i]
                return carry
            lax.fori_loop(0, count, fill, 0, unroll=4)

        def none(i, carry):
            ext[dz * wide * count + i] = jnp.zeros((slab, LANES), jnp.bfloat16)
            return carry

        if dz == 0:
            for l in range(1, wide):
                @pl.when(q < l)
                def _():
                    one(l)
        else:
            @pl.when(exists(dz))
            def _():
                for l in range(wide):
                    one(l)

            @pl.when(jnp.logical_not(exists(dz)))
            def _():
                lax.fori_loop(0, wide * count, none, 0, unroll=4)

    def reached(dz):
        if dz < 0:
            return 0
        if dz == depth:
            return pairs
        return jnp.clip((dz + 1) * wide - q - 1, 0, pairs)

    def multiply(dz):
        def pair(k, carry):
            shift = offsets_ref[k]

            def channel(i, inner):
                place = me * count + i + shift
                keep = jnp.where(place < total, 1.0 / windows, 0.0)
                near = jnp.minimum(q * count + i + shift, ext.shape[0] - 1)
                partner = ext[near].astype(jnp.float32)
                straight = own[i, :8] * partner[:8]
                twisted = swapped[i, :8] * partner[:8]
                for w in range(1, windows):
                    part = slice(w * 8, w * 8 + 8)
                    straight += own[i, part] * partner[part]
                    twisted += swapped[i, part] * partner[part]
                joined = jnp.where(
                    low,
                    straight + pltpu.roll(straight, 4, 0),
                    pltpu.roll(twisted, 4, 0) - twisted,
                )
                cross_ref[i, k] = joined * keep
                return inner

            return lax.fori_loop(0, count, channel, carry, unroll=4)

        lax.fori_loop(reached(dz - 1), reached(dz), pair, 0)

    sends(0)
    lax.fori_loop(0, count, prepare, 0)
    for dz in range(depth + 1):
        if dz < depth:
            sends(dz + 1)
        passes(dz)
        arrives(dz)
        settle(dz)
        multiply(dz)
    for dz in range(depth + 1):
        finishes(dz)


def shards(columns, records, live_mask, offsets):
    count, windows, length = records.shape
    pairs = offsets.shape[0]
    wide = 2 * columns
    layers = lax.axis_size("chan") // wide
    reach = (BAND + count - 2) // count
    depth = min(layers - 1, (wide - 1 + reach) // wide)
    pieces = PIECES
    spectra = whiten(records, live_mask).reshape(count, windows * 8, LANES)
    slots = (depth + 1) * wide
    cross = pl.pallas_call(
        functools.partial(reach_kernel, (layers, columns, depth, pieces, windows)),
        out_shape=jax.ShapeDtypeStruct((count, pairs, 8, LANES), jnp.float32),
        in_specs=[
            pl.BlockSpec(memory_space=pltpu.SMEM),
            pl.BlockSpec(memory_space=pltpu.VMEM),
        ],
        out_specs=pl.BlockSpec(memory_space=pltpu.VMEM),
        scratch_shapes=[
            pltpu.VMEM((slots, count, windows * 8, LANES), jnp.bfloat16),
            pltpu.VMEM((slots * count, windows * 8, LANES), jnp.bfloat16),
            pltpu.VMEM((count, windows * 8, LANES), jnp.float32),
            pltpu.VMEM((count, windows * 8, LANES), jnp.float32),
        ]
        + [pltpu.SemaphoreType.DMA((depth + 1, pieces))] * 8,
        compiler_params=pltpu.CompilerParams(
            vmem_limit_bytes=40 * 1024 * 1024, collective_id=0, has_side_effects=True
        ),
    )(offsets, spectra)
    cross = cross.astype(jnp.bfloat16).reshape(count * pairs, 8 * LANES)
    result = jnp.dot(cross, jnp.asarray(inverse_table(length)), preferred_element_type=jnp.float32)
    result = result * (1.0 / math.sqrt(F))
    return result.reshape(count, pairs, LAGS).astype(jnp.bfloat16)


def solution(mesh):
    in_specs = (P(("day", "chan"), None, None), P(("day", "chan")), P())
    out_specs = P(("day", "chan"), None, None)
    columns = max(1, LAYER_CHIPS // mesh.shape["day"])
    body = functools.partial(shards, columns)
    return jax.shard_map(body, mesh=mesh, in_specs=in_specs, out_specs=out_specs, check_vma=False)
```

time: 110 us -> 64.9 us (0.59)
  waiting for transfers between devices: 76.9 us -> 0 us
  Pallas kernels: 4.24 us -> 54.1 us
  between operations: 13.4 us -> 0.08 us
  local copies, waits for them, and re-layouts: 5.26 us -> 1.09 us
    all_gather x1 -> x0, waiting for transfers between devices: 76.9 us -> none  [shards(): gathered = lax.all_gather(spectra, 'chan', axis=0, tiled=True)]
    pallas_call x1, Pallas kernels: 4.24 us -> 54.1 us  [shards(): pl.pallas_call(functools.partial(reach_kernel, (layers, columns, depth, p...]
    unnamed x8 -> x6, local copies, waits for them, and re-layouts: 3.87 us -> 0.49 us
  transfers between devices with their start and end apart: 1 -> 0, of which waited for: 1 -> 0; matrix products, arithmetic and copies ran while one was open for 0% -> 0% of each run, Pallas kernels for 0% -> 0%
where the time goes in v2:
time: 64.9 us; the launch traced here: 64.7 us
  Pallas kernels  54.1 us (83%)
  matrix products  8.35 us (13%)
  local copies, waits for them, and re-layouts  1.09 us (2%)
  other arithmetic  1.05 us (2%)
    pallas_call x1, Pallas kernels, shards(): pl.pallas_call(functools.partial(reach_kernel, (layers, columns, depth, p...  54.1 us
    dot_general x1, matrix products, whiten(): jnp.dot(records.reshape(count * windows, length), jnp.asarray(forward_tab...  4.69 us
    dot_general x1, matrix products, shards(): jnp.dot(cross, jnp.asarray(inverse_table(length)), preferred_element_type...  3.66 us

profile of v2, /device:TPU:1, one launch (start us, length us, event | category | flops | bytes accessed | tf_op | source)
XLA Modules:
  0.0 64.7 jit_solution(17832499316319125593)
XLA Ops:
  0.0 0.0 copy-start
  0.0 0.8 %convert_element_type.15 = f32[32]{0:T(128)S(1)} convert(s32[32]{0:T(128)} %param.6) | non-fusion elementwise | flops 32 | bytes 256 | tf_op jit(solution)/shard_map/convert_element_type | solution.py:45
  0.8 0.1 broadcast_in_dim.4
  0.9 0.1 broadcast_in_dim_reshape.3
  0.9 0.5 copy-done
  1.4 0.0 copy-start.1
  1.4 4.7 %multiply_reduce_fusion = (f32[256]{0:T(256)S(1)}, f32[1024,256]{1,0:T(8,128)S(1)}) fusion(bf16[3000,1024]{1,0:T(8,128)(2,1)} %constant.13.clone, bf16[32,8,3000]{2,1,0:T(8,128)(2,1)S(1)} %copy-done), kind=kOutput, calls=%fused_computation.6 | convolution fusion | flops 1573388032 | bytes 8729600 | tf_op jit(solution)/shard_map/dot_general | solution.py:39
  6.1 0.1 fusion.4
  6.2 0.2 copy.7
  6.5 0.2 reshape.27.white_ref
  6.7 0.0 copy-done.1
  6.7 0.0 copy-start.2
  6.7 54.1 %shard_map.55 = f32[32,16,8,128]{3,2,1,0:T(8,128)S(1)} custom-call(s32[16]{0:T(128)S(1)} %copy-done.1, bf16[32,64,128]{2,1,0:T(8,128)(2,1)S(1)} %reshape.27.white_ref), custom_call_target="tpu_custom_call" | custom-call | tf_op jit(solution)/shard_map/pallas_call | solution.py:274
  60.9 0.2 convert_element_type.17
  61.0 0.0 copy-done.2
  61.0 3.7 %multiply_convert_fusion = bf16[512,2048]{1,0:T(8,128)(2,1)} fusion(bf16[1024,2048]{1,0:T(8,128)(2,1)S(1)} %copy-done.2, bf16[64,8,8,128]{3,2,1,0:T(8,128)(2,1)S(1)} %bitcast.15), kind=kOutput, calls=%fused_computation | convolution fusion | flops 2149580800 | bytes 7340032 | tf_op jit(solution)/shard_map/dot_general | solution.py:294
  (1 shorter events, 0.0 us)
Async XLA Ops:
  0.0 1.4 %copy-start = (bf16[32,8,3000]{2,1,0:T(8,128)(2,1)S(1)}, bf16[32,8,3000]{2,1,0:T(8,128)(2,1)}, u32[]{:S(2)}) copy-start(bf16[32,8,3000]{2,1,0:T(8,128)(2,1)} %param.5) | copy-start | bytes 4608004
  1.4 5.3 %copy-start.1 = (s32[16]{0:T(128)S(1)}, s32[16]{0:T(128)}, u32[]{:S(2)}) copy-start(s32[16]{0:T(128)} %offsets_ref.1) | copy-start | bytes 196
  6.7 54.3 %copy-start.2 = (bf16[1024,2048]{1,0:T(8,128)(2,1)S(1)}, bf16[1024,2048]{1,0:T(8,128)(2,1)}, u32[]{:S(2)}) copy-start(bf16[1024,2048]{1,0:T(8,128)(2,1)} %constant.14.clone) | copy-start | bytes 12582916

commit v3 on v2

--- a/solution.py
+++ b/solution.py
@@ -48,7 +48,7 @@
 
 
 def reach_kernel(shape, offsets_ref, white_ref, cross_ref, held, ext, own, swapped,
-                 z_send, z_recv, c_send, c_recv, y_send, y_recv, d_send, d_recv):
+                 z_send, z_recv, c_send, c_recv, y_send, y_recv, d_send, d_recv, e_send):
     layers, columns, depth, pieces, windows = shape
     count, slab = white_ref.shape[0], white_ref.shape[1]
     pairs = offsets_ref.shape[0]
@@ -124,6 +124,28 @@
     def exists(dz):
         return z + dz < layers
 
+    def last(dz):
+        return z + dz == layers - 1
+
+    detours = columns == 2 and depth == layers - 1
+
+    def detoured(dz, p):
+        return detours and dz > 0 and p >= pieces - pieces // 2
+
+    def goes_over(dz, p):
+        if dz == 0:
+            return both(exists(dz), y == 1)
+        if detoured(dz, p):
+            return both(exists(dz), jnp.logical_not(both(last(dz), y == 1)))
+        return exists(dz)
+
+    def extra(dz, p):
+        return copy(held.at[dz * wide + mate_q, rows(p)], (dz + 1) * wide + mate_q, p,
+                    e_send.at[dz, p], y_recv.at[dz + 1, p], me - wide)
+
+    def goes_extra(dz):
+        return both(last(dz), y == 0, z >= 1)
+
     def sends(dz):
         for p in range(pieces):
             if dz > 0:
@@ -135,7 +157,7 @@
                 def _():
                     down(dz, p).start()
             if columns == 2:
-                @pl.when(both(exists(dz), y == 1) if dz == 0 else exists(dz))
+                @pl.when(goes_over(dz, p))
                 def _():
                     over(dz, p, dz * wide + q).start()
             @pl.when(both(exists(dz), c == 1) if dz == 0 else exists(dz))
@@ -149,6 +171,10 @@
                 def _():
                     over(dz, p, dz * wide + mate_q).wait_recv()
                     onward(dz, p, dz * wide + mate_q).start()
+                if dz < depth and detoured(dz + 1, p):
+                    @pl.when(goes_extra(dz))
+                    def _():
+                        extra(dz, p).start()
 
     def arrives(dz):
         for p in range(pieces):
@@ -167,9 +193,13 @@
                 def _():
                     down(dz, p).wait_send()
             if columns == 2:
-                @pl.when(both(exists(dz), y == 1) if dz == 0 else exists(dz))
+                @pl.when(goes_over(dz, p))
                 def _():
                     over(dz, p, dz * wide + q).wait_send()
+                if dz < depth and detoured(dz + 1, p):
+                    @pl.when(goes_extra(dz))
+                    def _():
+                        extra(dz, p).wait_send()
                 @pl.when(both(exists(dz), y == 0) if dz == 0 else exists(dz))
                 def _():
                     onward(dz, p, dz * wide + mate_q).wait_send()
@@ -285,7 +315,7 @@
             pltpu.VMEM((count, windows * 8, LANES), jnp.float32),
             pltpu.VMEM((count, windows * 8, LANES), jnp.float32),
         ]
-        + [pltpu.SemaphoreType.DMA((depth + 1, pieces))] * 8,
+        + [pltpu.SemaphoreType.DMA((depth + 1, pieces))] * 9,
         compiler_params=pltpu.CompilerParams(
             vmem_limit_bytes=40 * 1024 * 1024, collective_id=0, has_side_effects=True
         ),

time: 64.9 us -> 59.8 us (0.921)
  Pallas kernels: 54.1 us -> 49.1 us
    pallas_call x1, Pallas kernels: 54.1 us -> 49.1 us  [shards(): pl.pallas_call(functools.partial(reach_kernel, (layers, columns, depth, p...]
where the time goes in v3:
time: 59.8 us; the launch traced here: 59.6 us
  Pallas kernels  49.1 us (82%)
  matrix products  8.35 us (14%)
  local copies, waits for them, and re-layouts  1.09 us (2%)
  other arithmetic  1.05 us (2%)
    pallas_call x1, Pallas kernels, shards(): pl.pallas_call(functools.partial(reach_kernel, (layers, columns, depth, p...  49.1 us
    dot_general x1, matrix products, whiten(): jnp.dot(records.reshape(count * windows, length), jnp.asarray(forward_tab...  4.69 us
    dot_general x1, matrix products, shards(): jnp.dot(cross, jnp.asarray(inverse_table(length)), preferred_element_type...  3.66 us

profile of v3, /device:TPU:1, one launch (start us, length us, event | category | flops | bytes accessed | tf_op | source)
XLA Modules:
  0.0 59.6 jit_solution(14186880466665901350)
XLA Ops:
  0.0 0.0 copy-start
  0.0 0.8 %convert_element_type.15 = f32[32]{0:T(128)S(1)} convert(s32[32]{0:T(128)} %param.6) | non-fusion elementwise | flops 32 | bytes 256 | tf_op jit(solution)/shard_map/convert_element_type | solution.py:45
  0.8 0.1 broadcast_in_dim.4
  0.9 0.1 broadcast_in_dim_reshape.3
  0.9 0.5 copy-done
  1.4 0.0 copy-start.1
  1.4 4.7 %multiply_reduce_fusion = (f32[256]{0:T(256)S(1)}, f32[1024,256]{1,0:T(8,128)S(1)}) fusion(bf16[3000,1024]{1,0:T(8,128)(2,1)} %constant.13.clone, bf16[32,8,3000]{2,1,0:T(8,128)(2,1)S(1)} %copy-done), kind=kOutput, calls=%fused_computation.6 | convolution fusion | flops 1573388032 | bytes 8729600 | tf_op jit(solution)/shard_map/dot_general | solution.py:39
  6.1 0.1 fusion.4
  6.2 0.2 copy.7
  6.5 0.2 reshape.27.white_ref
  6.7 0.0 copy-done.1
  6.7 0.0 copy-start.2
  6.7 49.1 %shard_map.55 = f32[32,16,8,128]{3,2,1,0:T(8,128)S(1)} custom-call(s32[16]{0:T(128)S(1)} %copy-done.1, bf16[32,64,128]{2,1,0:T(8,128)(2,1)S(1)} %reshape.27.white_ref), custom_call_target="tpu_custom_call" | custom-call | tf_op jit(solution)/shard_map/pallas_call | solution.py:304
  55.8 0.2 convert_element_type.17
  55.9 0.0 copy-done.2
  56.0 3.7 %multiply_convert_fusion = bf16[512,2048]{1,0:T(8,128)(2,1)} fusion(bf16[1024,2048]{1,0:T(8,128)(2,1)S(1)} %copy-done.2, bf16[64,8,8,128]{3,2,1,0:T(8,128)(2,1)S(1)} %bitcast.15), kind=kOutput, calls=%fused_computation | convolution fusion | flops 2149580800 | bytes 7340032 | tf_op jit(solution)/shard_map/dot_general | solution.py:324
  (1 shorter events, 0.0 us)
Async XLA Ops:
  0.0 1.4 %copy-start = (bf16[32,8,3000]{2,1,0:T(8,128)(2,1)S(1)}, bf16[32,8,3000]{2,1,0:T(8,128)(2,1)}, u32[]{:S(2)}) copy-start(bf16[32,8,3000]{2,1,0:T(8,128)(2,1)} %param.5) | copy-start | bytes 4608004
  1.4 5.3 %copy-start.1 = (s32[16]{0:T(128)S(1)}, s32[16]{0:T(128)}, u32[]{:S(2)}) copy-start(s32[16]{0:T(128)} %offsets_ref.1) | copy-start | bytes 196
  6.7 49.2 %copy-start.2 = (bf16[1024,2048]{1,0:T(8,128)(2,1)S(1)}, bf16[1024,2048]{1,0:T(8,128)(2,1)}, u32[]{:S(2)}) copy-start(bf16[1024,2048]{1,0:T(8,128)(2,1)} %constant.14.clone) | copy-start | bytes 12582916

commit v4 on v2

--- a/solution.py
+++ b/solution.py
@@ -47,9 +47,9 @@
     return white.astype(jnp.bfloat16)
 
 
-def reach_kernel(shape, offsets_ref, white_ref, cross_ref, held, ext, own, swapped,
-                 z_send, z_recv, c_send, c_recv, y_send, y_recv, d_send, d_recv):
-    layers, columns, depth, pieces, windows = shape
+def reach_kernel(shape, offsets_ref, white_ref, cross_ref, held, ext, own, swapped, made, back,
+                 z_send, z_recv, c_send, c_recv, y_send, y_recv, d_send, d_recv, r_send, r_recv):
+    layers, columns, depth, pieces, windows, fold = shape
     count, slab = white_ref.shape[0], white_ref.shape[1]
     pairs = offsets_ref.shape[0]
     wide = 2 * columns
@@ -63,6 +63,7 @@
     mate_q = q + 2 - 4 * y
     far_q = sib_q + 2 - 4 * y
     step = count // pieces
+    top, lifted = layers - 1, depth + 1
 
     barrier = pltpu.get_barrier_semaphore()
 
@@ -81,8 +82,21 @@
     def _():
         greet(me + wide)
 
-    above = jnp.minimum(layers - 1 - z, 1)
-    pl.semaphore_wait(barrier, columns + jnp.minimum(z, 1) + above)
+    below, above = jnp.minimum(z, 1), jnp.minimum(top - z, 1)
+    peers = columns + below + above
+    if fold:
+        @pl.when(z == 0)
+        def _():
+            for i in range(wide):
+                greet(top * wide + i)
+
+        @pl.when(z == top)
+        def _():
+            for i in range(wide):
+                greet(jnp.int32(i))
+
+        peers = peers + wide * (2 - below - above)
+    pl.semaphore_wait(barrier, peers)
 
     def rows(p):
         return pl.ds(p * step, step)
@@ -124,58 +138,114 @@
     def exists(dz):
         return z + dz < layers
 
+    def goes(dz, at_start, at_end):
+        if dz == lifted:
+            return z == top
+        if dz == 0:
+            return at_start
+        if fold and dz == depth:
+            return both(exists(dz), at_end)
+        return exists(dz)
+
+    def z_tx(dz):
+        if fold and dz + 1 == depth:
+            return both(exists(dz), z >= 1, jnp.logical_or(z >= 2, q == 0))
+        return both(exists(dz), z >= 1)
+
+    def z_rx(dz):
+        return goes(dz, None, q == 0)
+
+    def c_tx(dz):
+        return goes(dz, c == 1, q == 0)
+
+    def c_rx(dz):
+        return goes(dz, c == 0, q == 1)
+
+    def y_tx(dz):
+        return goes(dz, y == 1, q == 0)
+
+    def y_rx(dz):
+        return goes(dz, y == 0, q == 2)
+
+    def d_rx(dz):
+        return goes(dz, y == 0, q == 3)
+
+    def lift(p):
+        return copy(white_ref.at[rows(p)], lifted * wide + q, p, z_send.at[lifted, p], z_recv.at[lifted, p],
+                    me + top * wide)
+
     def sends(dz):
         for p in range(pieces):
             if dz > 0:
-                @pl.when(exists(dz))
+                @pl.when(z_rx(dz))
                 def _():
                     from_above(dz, p).wait_recv()
             if dz < depth:
-                @pl.when(both(exists(dz), z >= 1))
+                @pl.when(z_tx(dz))
                 def _():
                     down(dz, p).start()
             if columns == 2:
-                @pl.when(both(exists(dz), y == 1) if dz == 0 else exists(dz))
+                @pl.when(y_tx(dz))
                 def _():
                     over(dz, p, dz * wide + q).start()
-            @pl.when(both(exists(dz), c == 1) if dz == 0 else exists(dz))
+            @pl.when(c_tx(dz))
             def _():
                 across(dz, p, dz * wide + q).start()
 
     def passes(dz):
         if columns == 2:
             for p in range(pieces):
-                @pl.when(both(exists(dz), y == 0) if dz == 0 else exists(dz))
+                @pl.when(y_rx(dz))
                 def _():
                     over(dz, p, dz * wide + mate_q).wait_recv()
                     onward(dz, p, dz * wide + mate_q).start()
 
     def arrives(dz):
         for p in range(pieces):
-            @pl.when(both(exists(dz), c == 0) if dz == 0 else exists(dz))
+            @pl.when(c_rx(dz))
             def _():
                 across(dz, p, dz * wide + sib_q).wait_recv()
             if columns == 2:
-                @pl.when(both(exists(dz), y == 0) if dz == 0 else exists(dz))
+                @pl.when(d_rx(dz))
                 def _():
                     onward(dz, p, dz * wide + far_q).wait_recv()
 
     def finishes(dz):
         for p in range(pieces):
             if dz < depth:
-                @pl.when(both(exists(dz), z >= 1))
+                @pl.when(z_tx(dz))
                 def _():
                     down(dz, p).wait_send()
             if columns == 2:
-                @pl.when(both(exists(dz), y == 1) if dz == 0 else exists(dz))
+                @pl.when(y_tx(dz))
                 def _():
                     over(dz, p, dz * wide + q).wait_send()
-                @pl.when(both(exists(dz), y == 0) if dz == 0 else exists(dz))
+                @pl.when(y_rx(dz))
                 def _():
                     onward(dz, p, dz * wide + mate_q).wait_send()
-            @pl.when(both(exists(dz), c == 1) if dz == 0 else exists(dz))
+            @pl.when(c_tx(dz))
             def _():
                 across(dz, p, dz * wide + q).wait_send()
+
+    def answer(i):
+        return pltpu.make_async_remote_copy(
+            src_ref=made.at[i],
+            dst_ref=back.at[q],
+            send_sem=r_send.at[i],
+            recv_sem=r_recv.at[q],
+            device_id={"chan": jnp.int32(i)},
+            device_id_type=pl.DeviceIdType.MESH,
+        )
+
+    def answered(i):
+        return pltpu.make_async_remote_copy(
+            src_ref=made.at[i],
+            dst_ref=back.at[i],
+            send_sem=r_send.at[i],
+            recv_sem=r_recv.at[i],
+            device_id={"chan": me},
+            device_id_type=pl.DeviceIdType.MESH,
+        )
 
     low = lax.broadcasted_iota(jnp.int32, (8, LANES), 0) < 4
 
@@ -207,7 +277,7 @@
         else:
             @pl.when(exists(dz))
             def _():
-                for l in range(wide):
+                for l in range(1 if fold and dz == depth else wide):
                     one(l)
 
             @pl.when(jnp.logical_not(exists(dz)))
@@ -246,17 +316,104 @@
 
             return lax.fori_loop(0, count, channel, carry, unroll=4)
 
-        lax.fori_loop(reached(dz - 1), reached(dz), pair, 0)
+        begin, end = reached(dz - 1), reached(dz)
+        if fold and dz == depth:
+            @pl.when(z == 0)
+            def _():
+                lax.fori_loop(begin, begin + 1, pair, 0)
+
+            @pl.when(z > 0)
+            def _():
+                lax.fori_loop(begin, end, pair, 0)
+        else:
+            lax.fori_loop(begin, end, pair, 0)
+
+    def reply():
+        for i in range(wide):
+            shift = offsets_ref[top * wide + q - i]
+
+            def channel(r, carry):
+                place = i * count + r + shift
+                keep = jnp.where(place < total, 1.0 / windows, 0.0)
+                near = jnp.clip(place - top * wide * count, 0, ext.shape[0] - 1)
+                partner = ext[near].astype(jnp.float32)
+                value = held[lifted * wide + i, r].astype(jnp.float32)
+                straight = value[:8] * partner[:8]
+                twisted = pltpu.roll(value[:8], 4, 0) * partner[:8]
+                for w in range(1, windows):
+                    part = slice(w * 8, w * 8 + 8)
+                    straight += value[part] * partner[part]
+                    twisted += pltpu.roll(value[part], 4, 0) * partner[part]
+                joined = jnp.where(
+                    low,
+                    straight + pltpu.roll(straight, 4, 0),
+                    pltpu.roll(twisted, 4, 0) - twisted,
+                )
+                made[i, r] = (joined * keep).astype(jnp.bfloat16)
+                return carry
+
+            lax.fori_loop(0, count, channel, 0, unroll=4)
+        for i in range(wide):
+            answer(i).start()
 
     sends(0)
+    if fold:
+        @pl.when(z == 0)
+        def _():
+            for p in range(pieces):
+                lift(p).start()
+
     lax.fori_loop(0, count, prepare, 0)
     for dz in range(depth + 1):
         if dz < depth:
             sends(dz + 1)
+        if fold and dz == 0:
+            sends(lifted)
         passes(dz)
+        if fold and dz == 0:
+            passes(lifted)
         arrives(dz)
         settle(dz)
+        if fold and dz == 0:
+            arrives(lifted)
+
+            @pl.when(z == top)
+            def _():
+                def blank(i, carry):
+                    ext[wide * count + i] = jnp.zeros((slab, LANES), jnp.bfloat16)
+                    return carry
+
+                lax.fori_loop(0, 2 * count, blank, 0, unroll=4)
+                reply()
+
         multiply(dz)
+
+    if fold:
+        @pl.when(z == 0)
+        def _():
+            def nothing(k, carry):
+                for r in range(count):
+                    cross_ref[r, k] = jnp.zeros((8, LANES), jnp.float32)
+                return carry
+
+            lax.fori_loop(pairs - q, pairs, nothing, 0)
+            for i in range(wide):
+                answered(i).wait_recv()
+
+                def take(r, carry):
+                    cross_ref[r, top * wide - q + i] = back[i, r].astype(jnp.float32)
+                    return carry
+
+                lax.fori_loop(0, count, take, 0, unroll=4)
+            for p in range(pieces):
+                lift(p).wait_send()
+
+        @pl.when(z == top)
+        def _():
+            for i in range(wide):
+                answer(i).wait_send()
+
+        finishes(lifted)
     for dz in range(depth + 1):
         finishes(dz)
 
@@ -269,10 +426,11 @@
     reach = (BAND + count - 2) // count
     depth = min(layers - 1, (wide - 1 + reach) // wide)
     pieces = PIECES
+    fold = columns == 2 and depth == layers - 1 and depth >= 2 and layers * wide == pairs and pairs * count == BAND
     spectra = whiten(records, live_mask).reshape(count, windows * 8, LANES)
     slots = (depth + 1) * wide
     cross = pl.pallas_call(
-        functools.partial(reach_kernel, (layers, columns, depth, pieces, windows)),
+        functools.partial(reach_kernel, (layers, columns, depth, pieces, windows, fold)),
         out_shape=jax.ShapeDtypeStruct((count, pairs, 8, LANES), jnp.float32),
         in_specs=[
             pl.BlockSpec(memory_space=pltpu.SMEM),
@@ -280,12 +438,15 @@
         ],
         out_specs=pl.BlockSpec(memory_space=pltpu.VMEM),
         scratch_shapes=[
-            pltpu.VMEM((slots, count, windows * 8, LANES), jnp.bfloat16),
+            pltpu.VMEM((slots + wide, count, windows * 8, LANES), jnp.bfloat16),
             pltpu.VMEM((slots * count, windows * 8, LANES), jnp.bfloat16),
             pltpu.VMEM((count, windows * 8, LANES), jnp.float32),
             pltpu.VMEM((count, windows * 8, LANES), jnp.float32),
+            pltpu.VMEM((wide, count, 8, LANES), jnp.bfloat16),
+            pltpu.VMEM((wide, count, 8, LANES), jnp.bfloat16),
         ]
-        + [pltpu.SemaphoreType.DMA((depth + 1, pieces))] * 8,
+        + [pltpu.SemaphoreType.DMA((depth + 2, pieces))] * 8
+        + [pltpu.SemaphoreType.DMA((wide,))] * 2,
         compiler_params=pltpu.CompilerParams(
             vmem_limit_bytes=40 * 1024 * 1024, collective_id=0, has_side_effects=True
         ),

time: 64.9 us -> 59.4 us (0.915)
  Pallas kernels: 54.1 us -> 48.6 us
    pallas_call x1, Pallas kernels: 54.1 us -> 48.6 us  [shards(): pl.pallas_call(functools.partial(reach_kernel, (layers, columns, depth, p...]
where the time goes in v4:
time: 59.4 us; the launch traced here: 59.2 us
  Pallas kernels  48.6 us (82%)
  matrix products  8.35 us (14%)
  local copies, waits for them, and re-layouts  1.09 us (2%)
  other arithmetic  1.05 us (2%)
    pallas_call x1, Pallas kernels, shards(): pl.pallas_call(functools.partial(reach_kernel, (layers, columns, depth, p...  48.6 us
    dot_general x1, matrix products, whiten(): jnp.dot(records.reshape(count * windows, length), jnp.asarray(forward_tab...  4.69 us
    dot_general x1, matrix products, shards(): jnp.dot(cross, jnp.asarray(inverse_table(length)), preferred_element_type...  3.66 us

profile of v4, /device:TPU:1, one launch (start us, length us, event | category | flops | bytes accessed | tf_op | source)
XLA Modules:
  0.0 59.2 jit_solution(14305302398120539849)
XLA Ops:
  0.0 0.0 copy-start
  0.0 0.8 %convert_element_type.15 = f32[32]{0:T(128)S(1)} convert(s32[32]{0:T(128)} %param.6) | non-fusion elementwise | flops 32 | bytes 256 | tf_op jit(solution)/shard_map/convert_element_type | solution.py:45
  0.8 0.1 broadcast_in_dim.4
  0.9 0.1 broadcast_in_dim_reshape.3
  0.9 0.5 copy-done
  1.4 0.0 copy-start.1
  1.4 4.7 %multiply_reduce_fusion = (f32[256]{0:T(256)S(1)}, f32[1024,256]{1,0:T(8,128)S(1)}) fusion(bf16[3000,1024]{1,0:T(8,128)(2,1)} %constant.13.clone, bf16[32,8,3000]{2,1,0:T(8,128)(2,1)S(1)} %copy-done), kind=kOutput, calls=%fused_computation.6 | convolution fusion | flops 1573388032 | bytes 8729600 | tf_op jit(solution)/shard_map/dot_general | solution.py:39
  6.1 0.1 fusion.4
  6.2 0.2 copy.7
  6.5 0.2 reshape.27.white_ref
  6.7 0.0 copy-done.1
  6.7 0.0 copy-start.2
  6.7 48.6 %shard_map.55 = f32[32,16,8,128]{3,2,1,0:T(8,128)S(1)} custom-call(s32[16]{0:T(128)S(1)} %copy-done.1, bf16[32,64,128]{2,1,0:T(8,128)(2,1)S(1)} %reshape.27.white_ref), custom_call_target="tpu_custom_call" | custom-call | tf_op jit(solution)/shard_map/pallas_call | solution.py:432
  55.4 0.2 convert_element_type.17
  55.5 0.0 copy-done.2
  55.6 3.7 %multiply_convert_fusion = bf16[512,2048]{1,0:T(8,128)(2,1)} fusion(bf16[1024,2048]{1,0:T(8,128)(2,1)S(1)} %copy-done.2, bf16[64,8,8,128]{3,2,1,0:T(8,128)(2,1)S(1)} %bitcast.15), kind=kOutput, calls=%fused_computation | convolution fusion | flops 2149580800 | bytes 7340032 | tf_op jit(solution)/shard_map/dot_general | solution.py:455
  (1 shorter events, 0.0 us)
Async XLA Ops:
  0.0 1.4 %copy-start = (bf16[32,8,3000]{2,1,0:T(8,128)(2,1)S(1)}, bf16[32,8,3000]{2,1,0:T(8,128)(2,1)}, u32[]{:S(2)}) copy-start(bf16[32,8,3000]{2,1,0:T(8,128)(2,1)} %param.5) | copy-start | bytes 4608004
  1.4 5.3 %copy-start.1 = (s32[16]{0:T(128)S(1)}, s32[16]{0:T(128)}, u32[]{:S(2)}) copy-start(s32[16]{0:T(128)} %offsets_ref.1) | copy-start | bytes 196
  6.7 48.8 %copy-start.2 = (bf16[1024,2048]{1,0:T(8,128)(2,1)S(1)}, bf16[1024,2048]{1,0:T(8,128)(2,1)}, u32[]{:S(2)}) copy-start(bf16[1024,2048]{1,0:T(8,128)(2,1)} %constant.14.clone) | copy-start | bytes 12582916

commit v5 on v4

--- a/solution.py
+++ b/solution.py
@@ -265,10 +265,6 @@
                 return carry
             lax.fori_loop(0, count, fill, 0, unroll=4)
 
-        def none(i, carry):
-            ext[dz * wide * count + i] = jnp.zeros((slab, LANES), jnp.bfloat16)
-            return carry
-
         if dz == 0:
             for l in range(1, wide):
                 @pl.when(q < l)
@@ -280,16 +276,30 @@
                 for l in range(1 if fold and dz == depth else wide):
                     one(l)
 
-            @pl.when(jnp.logical_not(exists(dz)))
-            def _():
-                lax.fori_loop(0, wide * count, none, 0, unroll=4)
+    live = jnp.minimum(layers * wide - me, pairs)
+
+    def outside():
+        def nothing(k, carry):
+            for r in range(count):
+                cross_ref[r, k] = jnp.zeros((8, LANES), jnp.float32)
+            return carry
+
+        lax.fori_loop(live, pairs, nothing, 0)
+
+        @pl.when(layers - z <= depth)
+        def _():
+            def blank(i, carry):
+                ext[(layers - z) * wide * count + i] = jnp.zeros((slab, LANES), jnp.bfloat16)
+                return carry
+
+            lax.fori_loop(0, 2 * count, blank, 0, unroll=4)
 
     def reached(dz):
         if dz < 0:
             return 0
         if dz == depth:
-            return pairs
-        return jnp.clip((dz + 1) * wide - q - 1, 0, pairs)
+            return live
+        return jnp.minimum((dz + 1) * wide - q - 1, live)
 
     def multiply(dz):
         def pair(k, carry):
@@ -364,6 +374,7 @@
                 lift(p).start()
 
     lax.fori_loop(0, count, prepare, 0)
+    outside()
     for dz in range(depth + 1):
         if dz < depth:
             sends(dz + 1)
@@ -379,11 +390,6 @@
 
             @pl.when(z == top)
             def _():
-                def blank(i, carry):
-                    ext[wide * count + i] = jnp.zeros((slab, LANES), jnp.bfloat16)
-                    return carry
-
-                lax.fori_loop(0, 2 * count, blank, 0, unroll=4)
                 reply()
 
         multiply(dz)
@@ -391,12 +397,6 @@
     if fold:
         @pl.when(z == 0)
         def _():
-            def nothing(k, carry):
-                for r in range(count):
-                    cross_ref[r, k] = jnp.zeros((8, LANES), jnp.float32)
-                return carry
-
-            lax.fori_loop(pairs - q, pairs, nothing, 0)
             for i in range(wide):
                 answered(i).wait_recv()
 

time: 59.4 us -> 59.4 us (level)
  no operation moved by 1% of the time
where the time goes in v5:
time: 59.4 us; the launch traced here: 59.2 us
  Pallas kernels  48.6 us (82%)
  matrix products  8.35 us (14%)
  local copies, waits for them, and re-layouts  1.09 us (2%)
  other arithmetic  1.05 us (2%)
    pallas_call x1, Pallas kernels, shards(): pl.pallas_call(functools.partial(reach_kernel, (layers, columns, depth, p...  48.6 us
    dot_general x1, matrix products, whiten(): jnp.dot(records.reshape(count * windows, length), jnp.asarray(forward_tab...  4.69 us
    dot_general x1, matrix products, shards(): jnp.dot(cross, jnp.asarray(inverse_table(length)), preferred_element_type...  3.66 us

profile of v5, /device:TPU:1, one launch (start us, length us, event | category | flops | bytes accessed | tf_op | source)
XLA Modules:
  0.0 59.2 jit_solution(494619673919410634)
XLA Ops:
  0.0 0.0 copy-start
  0.0 0.8 %convert_element_type.15 = f32[32]{0:T(128)S(1)} convert(s32[32]{0:T(128)} %param.6) | non-fusion elementwise | flops 32 | bytes 256 | tf_op jit(solution)/shard_map/convert_element_type | solution.py:45
  0.8 0.1 broadcast_in_dim.4
  0.9 0.1 broadcast_in_dim_reshape.3
  0.9 0.5 copy-done
  1.4 0.0 copy-start.1
  1.4 4.7 %multiply_reduce_fusion = (f32[256]{0:T(256)S(1)}, f32[1024,256]{1,0:T(8,128)S(1)}) fusion(bf16[3000,1024]{1,0:T(8,128)(2,1)} %constant.13.clone, bf16[32,8,3000]{2,1,0:T(8,128)(2,1)S(1)} %copy-done), kind=kOutput, calls=%fused_computation.6 | convolution fusion | flops 1573388032 | bytes 8729600 | tf_op jit(solution)/shard_map/dot_general | solution.py:39
  6.1 0.1 fusion.4
  6.2 0.2 copy.7
  6.5 0.2 reshape.27.white_ref
  6.7 0.0 copy-done.1
  6.7 0.0 copy-start.2
  6.7 48.6 %shard_map.55 = f32[32,16,8,128]{3,2,1,0:T(8,128)S(1)} custom-call(s32[16]{0:T(128)S(1)} %copy-done.1, bf16[32,64,128]{2,1,0:T(8,128)(2,1)S(1)} %reshape.27.white_ref), custom_call_target="tpu_custom_call" | custom-call | tf_op jit(solution)/shard_map/pallas_call | solution.py:432
  55.4 0.2 convert_element_type.17
  55.5 0.0 copy-done.2
  55.5 3.7 %multiply_convert_fusion = bf16[512,2048]{1,0:T(8,128)(2,1)} fusion(bf16[1024,2048]{1,0:T(8,128)(2,1)S(1)} %copy-done.2, bf16[64,8,8,128]{3,2,1,0:T(8,128)(2,1)S(1)} %bitcast.15), kind=kOutput, calls=%fused_computation | convolution fusion | flops 2149580800 | bytes 7340032 | tf_op jit(solution)/shard_map/dot_general | solution.py:455
  (1 shorter events, 0.0 us)
Async XLA Ops:
  0.0 1.4 %copy-start = (bf16[32,8,3000]{2,1,0:T(8,128)(2,1)S(1)}, bf16[32,8,3000]{2,1,0:T(8,128)(2,1)}, u32[]{:S(2)}) copy-start(bf16[32,8,3000]{2,1,0:T(8,128)(2,1)} %param.5) | copy-start | bytes 4608004
  1.4 5.3 %copy-start.1 = (s32[16]{0:T(128)S(1)}, s32[16]{0:T(128)}, u32[]{:S(2)}) copy-start(s32[16]{0:T(128)} %offsets_ref.1) | copy-start | bytes 196
  6.7 48.8 %copy-start.2 = (bf16[1024,2048]{1,0:T(8,128)(2,1)S(1)}, bf16[1024,2048]{1,0:T(8,128)(2,1)}, u32[]{:S(2)}) copy-start(bf16[1024,2048]{1,0:T(8,128)(2,1)} %constant.14.clone) | copy-start | bytes 12582916

commit v6 on v5

--- a/solution.py
+++ b/solution.py
@@ -14,7 +14,7 @@
 LAGS = 2048
 LANES = 128
 BAND = 512
-PIECES = 2
+PIECES = 4
 LAYER_CHIPS = 4
 
 
@@ -48,7 +48,7 @@
 
 
 def reach_kernel(shape, offsets_ref, white_ref, cross_ref, held, ext, own, swapped, made, back,
-                 z_send, z_recv, c_send, c_recv, y_send, y_recv, d_send, d_recv, r_send, r_recv):
+                 z_send, z_recv, c_send, c_recv, y_send, y_recv, d_send, d_recv, e_send, r_send, r_recv):
     layers, columns, depth, pieces, windows, fold = shape
     count, slab = white_ref.shape[0], white_ref.shape[1]
     pairs = offsets_ref.shape[0]
@@ -167,6 +167,21 @@
     def y_rx(dz):
         return goes(dz, y == 0, q == 2)
 
+    def detoured(dz, p):
+        return fold and dz == depth - 1 and p == pieces - 1
+
+    def over_tx(dz, p):
+        if detoured(dz, p):
+            return both(y_tx(dz), jnp.logical_or(z > 0, y == 0))
+        return y_tx(dz)
+
+    def extra(dz, p):
+        return copy(held.at[dz * wide + mate_q, rows(p)], (dz + 1) * wide + mate_q, p,
+                    e_send.at[dz, p], y_recv.at[dz + 1, p], me - wide)
+
+    def extra_tx():
+        return both(z == 1, y == 0)
+
     def d_rx(dz):
         return goes(dz, y == 0, q == 3)
 
@@ -185,7 +200,7 @@
                 def _():
                     down(dz, p).start()
             if columns == 2:
-                @pl.when(y_tx(dz))
+                @pl.when(over_tx(dz, p))
                 def _():
                     over(dz, p, dz * wide + q).start()
             @pl.when(c_tx(dz))
@@ -199,6 +214,10 @@
                 def _():
                     over(dz, p, dz * wide + mate_q).wait_recv()
                     onward(dz, p, dz * wide + mate_q).start()
+                if detoured(dz + 1, p):
+                    @pl.when(extra_tx())
+                    def _():
+                        extra(dz, p).start()
 
     def arrives(dz):
         for p in range(pieces):
@@ -217,9 +236,13 @@
                 def _():
                     down(dz, p).wait_send()
             if columns == 2:
-                @pl.when(y_tx(dz))
+                @pl.when(over_tx(dz, p))
                 def _():
                     over(dz, p, dz * wide + q).wait_send()
+                if detoured(dz + 1, p):
+                    @pl.when(extra_tx())
+                    def _():
+                        extra(dz, p).wait_send()
                 @pl.when(y_rx(dz))
                 def _():
                     onward(dz, p, dz * wide + mate_q).wait_send()
@@ -445,7 +468,7 @@
             pltpu.VMEM((wide, count, 8, LANES), jnp.bfloat16),
             pltpu.VMEM((wide, count, 8, LANES), jnp.bfloat16),
         ]
-        + [pltpu.SemaphoreType.DMA((depth + 2, pieces))] * 8
+        + [pltpu.SemaphoreType.DMA((depth + 2, pieces))] * 9
         + [pltpu.SemaphoreType.DMA((wide,))] * 2,
         compiler_params=pltpu.CompilerParams(
             vmem_limit_bytes=40 * 1024 * 1024, collective_id=0, has_side_effects=True

time: 59.4 us -> 58.5 us (0.985); the launches traced: 59.2 us -> 57.4 us
  Pallas kernels: 48.6 us -> 46.8 us
    pallas_call x1, Pallas kernels: 48.6 us -> 46.8 us  [shards(): pl.pallas_call(functools.partial(reach_kernel, (layers, columns, depth, p...]
where the time goes in v6:
time: 58.5 us; the launch traced here: 57.4 us
  Pallas kernels  46.8 us (80%)
  matrix products  8.35 us (14%)
  local copies, waits for them, and re-layouts  1.09 us (2%)
  other arithmetic  1.05 us (2%)
    pallas_call x1, Pallas kernels, shards(): pl.pallas_call(functools.partial(reach_kernel, (layers, columns, depth, p...  46.8 us
    dot_general x1, matrix products, whiten(): jnp.dot(records.reshape(count * windows, length), jnp.asarray(forward_tab...  4.69 us
    dot_general x1, matrix products, shards(): jnp.dot(cross, jnp.asarray(inverse_table(length)), preferred_element_type...  3.66 us

profile of v6, /device:TPU:1, one launch (start us, length us, event | category | flops | bytes accessed | tf_op | source)
XLA Modules:
  0.0 57.4 jit_solution(14399969150709868038)
XLA Ops:
  0.0 0.0 copy-start
  0.0 0.8 %convert_element_type.15 = f32[32]{0:T(128)S(1)} convert(s32[32]{0:T(128)} %param.6) | non-fusion elementwise | flops 32 | bytes 256 | tf_op jit(solution)/shard_map/convert_element_type | solution.py:45
  0.8 0.1 broadcast_in_dim.4
  0.9 0.1 broadcast_in_dim_reshape.3
  0.9 0.5 copy-done
  1.4 0.0 copy-start.1
  1.4 4.7 %multiply_reduce_fusion = (f32[256]{0:T(256)S(1)}, f32[1024,256]{1,0:T(8,128)S(1)}) fusion(bf16[3000,1024]{1,0:T(8,128)(2,1)} %constant.13.clone, bf16[32,8,3000]{2,1,0:T(8,128)(2,1)S(1)} %copy-done), kind=kOutput, calls=%fused_computation.6 | convolution fusion | flops 1573388032 | bytes 8729600 | tf_op jit(solution)/shard_map/dot_general | solution.py:39
  6.1 0.1 fusion.4
  6.2 0.2 copy.7
  6.5 0.2 reshape.27.white_ref
  6.7 0.0 copy-done.1
  6.7 0.0 copy-start.2
  6.7 46.8 %shard_map.55 = f32[32,16,8,128]{3,2,1,0:T(8,128)S(1)} custom-call(s32[16]{0:T(128)S(1)} %copy-done.1, bf16[32,64,128]{2,1,0:T(8,128)(2,1)S(1)} %reshape.27.white_ref), custom_call_target="tpu_custom_call" | custom-call | tf_op jit(solution)/shard_map/pallas_call | solution.py:455
  53.6 0.2 convert_element_type.17
  53.7 0.0 copy-done.2
  53.7 3.7 %multiply_convert_fusion = bf16[512,2048]{1,0:T(8,128)(2,1)} fusion(bf16[1024,2048]{1,0:T(8,128)(2,1)S(1)} %copy-done.2, bf16[64,8,8,128]{3,2,1,0:T(8,128)(2,1)S(1)} %bitcast.15), kind=kOutput, calls=%fused_computation | convolution fusion | flops 2149580800 | bytes 7340032 | tf_op jit(solution)/shard_map/dot_general | solution.py:478
  (1 shorter events, 0.0 us)
Async XLA Ops:
  0.0 1.4 %copy-start = (bf16[32,8,3000]{2,1,0:T(8,128)(2,1)S(1)}, bf16[32,8,3000]{2,1,0:T(8,128)(2,1)}, u32[]{:S(2)}) copy-start(bf16[32,8,3000]{2,1,0:T(8,128)(2,1)} %param.5) | copy-start | bytes 4608004
  1.4 5.3 %copy-start.1 = (s32[16]{0:T(128)S(1)}, s32[16]{0:T(128)}, u32[]{:S(2)}) copy-start(s32[16]{0:T(128)} %offsets_ref.1) | copy-start | bytes 196
  6.7 47.0 %copy-start.2 = (bf16[1024,2048]{1,0:T(8,128)(2,1)S(1)}, bf16[1024,2048]{1,0:T(8,128)(2,1)}, u32[]{:S(2)}) copy-start(bf16[1024,2048]{1,0:T(8,128)(2,1)} %constant.14.clone) | copy-start | bytes 12582916

commit v7 on v6

--- a/solution.py
+++ b/solution.py
@@ -173,7 +173,16 @@
     def over_tx(dz, p):
         if detoured(dz, p):
             return both(y_tx(dz), jnp.logical_or(z > 0, y == 0))
+        if raised(dz, p):
+            return both(y_tx(dz), y == 0)
         return y_tx(dz)
+
+    def raised(dz, p):
+        return fold and dz == lifted and p >= pieces // 2
+
+    def lift_mate(p):
+        return copy(held.at[mate_q, rows(p)], lifted * wide + mate_q, p,
+                    e_send.at[lifted, p], y_recv.at[lifted, p], me + top * wide)
 
     def extra(dz, p):
         return copy(held.at[dz * wide + mate_q, rows(p)], (dz + 1) * wide + mate_q, p,
@@ -214,6 +223,10 @@
                 def _():
                     over(dz, p, dz * wide + mate_q).wait_recv()
                     onward(dz, p, dz * wide + mate_q).start()
+                if dz == 0 and raised(lifted, p):
+                    @pl.when(both(z == 0, y == 0))
+                    def _():
+                        lift_mate(p).start()
                 if detoured(dz + 1, p):
                     @pl.when(extra_tx())
                     def _():
@@ -430,6 +443,10 @@
                 lax.fori_loop(0, count, take, 0, unroll=4)
             for p in range(pieces):
                 lift(p).wait_send()
+                if raised(lifted, p):
+                    @pl.when(y == 0)
+                    def _():
+                        lift_mate(p).wait_send()
 
         @pl.when(z == top)
         def _():

time: 58.5 us -> 57.6 us (0.985); the launches traced: 57.4 us -> 57.4 us
  no operation moved by 1% of the time
where the time goes in v7:
time: 57.6 us; the launch traced here: 57.4 us
  Pallas kernels  46.9 us (81%)
  matrix products  8.35 us (14%)
  local copies, waits for them, and re-layouts  1.09 us (2%)
  other arithmetic  1.05 us (2%)
    pallas_call x1, Pallas kernels, shards(): pl.pallas_call(functools.partial(reach_kernel, (layers, columns, depth, p...  46.9 us
    dot_general x1, matrix products, whiten(): jnp.dot(records.reshape(count * windows, length), jnp.asarray(forward_tab...  4.69 us
    dot_general x1, matrix products, shards(): jnp.dot(cross, jnp.asarray(inverse_table(length)), preferred_element_type...  3.66 us

profile of v7, /device:TPU:1, one launch (start us, length us, event | category | flops | bytes accessed | tf_op | source)
XLA Modules:
  0.0 57.4 jit_solution(12340338501367269925)
XLA Ops:
  0.0 0.0 copy-start
  0.0 0.8 %convert_element_type.15 = f32[32]{0:T(128)S(1)} convert(s32[32]{0:T(128)} %param.6) | non-fusion elementwise | flops 32 | bytes 256 | tf_op jit(solution)/shard_map/convert_element_type | solution.py:45
  0.8 0.1 broadcast_in_dim.4
  0.9 0.1 broadcast_in_dim_reshape.3
  0.9 0.5 copy-done
  1.4 0.0 copy-start.1
  1.4 4.7 %multiply_reduce_fusion = (f32[256]{0:T(256)S(1)}, f32[1024,256]{1,0:T(8,128)S(1)}) fusion(bf16[3000,1024]{1,0:T(8,128)(2,1)} %constant.13.clone, bf16[32,8,3000]{2,1,0:T(8,128)(2,1)S(1)} %copy-done), kind=kOutput, calls=%fused_computation.6 | convolution fusion | flops 1573388032 | bytes 8729600 | tf_op jit(solution)/shard_map/dot_general | solution.py:39
  6.1 0.1 fusion.4
  6.2 0.2 copy.7
  6.5 0.2 reshape.27.white_ref
  6.7 0.0 copy-done.1
  6.7 0.0 copy-start.2
  6.7 46.9 %shard_map.55 = f32[32,16,8,128]{3,2,1,0:T(8,128)S(1)} custom-call(s32[16]{0:T(128)S(1)} %copy-done.1, bf16[32,64,128]{2,1,0:T(8,128)(2,1)S(1)} %reshape.27.white_ref), custom_call_target="tpu_custom_call" | custom-call | tf_op jit(solution)/shard_map/pallas_call | solution.py:472
  53.6 0.2 convert_element_type.17
  53.8 0.0 copy-done.2
  53.8 3.7 %multiply_convert_fusion = bf16[512,2048]{1,0:T(8,128)(2,1)} fusion(bf16[1024,2048]{1,0:T(8,128)(2,1)S(1)} %copy-done.2, bf16[64,8,8,128]{3,2,1,0:T(8,128)(2,1)S(1)} %bitcast.15), kind=kOutput, calls=%fused_computation | convolution fusion | flops 2149580800 | bytes 7340032 | tf_op jit(solution)/shard_map/dot_general | solution.py:495
  (1 shorter events, 0.0 us)
Async XLA Ops:
  0.0 1.4 %copy-start = (bf16[32,8,3000]{2,1,0:T(8,128)(2,1)S(1)}, bf16[32,8,3000]{2,1,0:T(8,128)(2,1)}, u32[]{:S(2)}) copy-start(bf16[32,8,3000]{2,1,0:T(8,128)(2,1)} %param.5) | copy-start | bytes 4608004
  1.4 5.3 %copy-start.1 = (s32[16]{0:T(128)S(1)}, s32[16]{0:T(128)}, u32[]{:S(2)}) copy-start(s32[16]{0:T(128)} %offsets_ref.1) | copy-start | bytes 196
  6.7 47.1 %copy-start.2 = (bf16[1024,2048]{1,0:T(8,128)(2,1)S(1)}, bf16[1024,2048]{1,0:T(8,128)(2,1)}, u32[]{:S(2)}) copy-start(bf16[1024,2048]{1,0:T(8,128)(2,1)} %constant.14.clone) | copy-start | bytes 12582916
